TPU v7x, 32 devices: a whole 2x2x4 slice. The times are simulated.
32 devices in a mesh: inst: 4 (over y, x), space: 8 (over z, core).
Axes of the slice: x: 2, y: 2, z: 4, core: 2. Of those that a mesh axis runs over, the one named last changes fastest.
Arguments:
- start_adjoint: float32 [32, 6, 64, 512], P('inst', None, 'space'), may hold values from -6 to 6
- adjoint_source: float32 [32, 6, 64, 512], P('inst', None, 'space'), may hold values from -48 to 48
- diagonal: float32 [6, 64, 512], P(None, 'space'), may hold values from 15 to 30
- flux_x: float32 [32, 6, 6, 64, 512], P('inst', None, None, 'space'), may hold values from -0.5 to 0.5
- flux_y: float32 [32, 6, 6, 64, 512], P('inst', None, None, 'space'), may hold values from -0.3 to 0.3
- shape_derivative: float32 [32, 6, 64, 512], P('inst', None, 'space'), may hold values from -6 to 6
- mode_basis: float32 [64, 512, 128], P('space'), may hold values from -0.0390625 to 0.0390625
- patch_of_cell: int32 [64, 512], P('space'), may hold values from 0 to 255, as said below
Outputs:
- adjoint: float32 [32, 6, 64, 512], P('inst', None, 'space')
- sensitivity: float32 [256, 128], P(('inst', 'space'))
Inputs may be any that keep to these rules, and one draw needn't show every extreme that they name: `patch_of_cell`: patch index of each cell; a cell's patch lies within 16 patches of the one at its position in the order of cells (x slowest).
All inputs are finite; a program needn't handle non-finite values.
Results may differ from a plain program's by a relative error of at most 0.0001.
Values sent between devices are 32-bit elements; how exact they have to be, the bound alone decides.
No kernel may reach another device: no remote copies, remote signals or barrier semaphores. Data moves between devices by JAX's collectives and lax.ppermute only.
A program may use at most 128 MiB of HBM per device.

v0:
```python
import jax
import jax.numpy as jnp
from jax import lax
from jax.sharding import PartitionSpec as P

NT = 32
SWEEPS = 2
PATCH_DEV = 8


spectral_scale = 0.1


def with_halo(cells, sides, width):
    for axis, dim in sides:
        count = lax.axis_size(axis)
        head = lax.slice_in_dim(cells, 0, width, axis=dim)
        tail = lax.slice_in_dim(cells, cells.shape[dim] - width, cells.shape[dim], axis=dim)
        cells = jnp.concatenate(
            [
                lax.ppermute(tail, axis, [(i, (i + 1) % count) for i in range(count)]),
                cells,
                lax.ppermute(head, axis, [((i + 1) % count, i) for i in range(count)]),
            ],
            axis=dim,
        )
    return cells


def spectral_weights(offset):
    angles = jnp.pi / NT * offset.astype(jnp.float32)
    parity = 1.0 - 2.0 * jnp.remainder(offset, 2).astype(jnp.float32)
    nonzero = offset != 0
    sine_value = jnp.where(nonzero, jnp.sin(angles), 1.0)
    return jnp.where(nonzero, 0.5 * parity * jnp.cos(angles) / sine_value, 0.0)


def apply_operator(
    adjoint, plus_one, minus_one, plus_two, minus_two, spectral, diagonal, flux_x, flux_y
):
    cell_above = jnp.pad(adjoint[..., 1:], ((0, 0), (0, 0), (0, 0), (0, 1)))
    cell_below = jnp.pad(adjoint[..., :-1], ((0, 0), (0, 0), (0, 0), (1, 0)))
    pitch_diff = 2.0 / 3.0 * (plus_one - minus_one) - 1.0 / 12.0 * (plus_two - minus_two)
    chord_diff = cell_above - cell_below
    transport = jnp.zeros_like(adjoint)
    for source in range(adjoint.shape[1]):
        transport = transport + flux_x[:, source] * pitch_diff[:, source : source + 1]
        transport = transport + flux_y[:, source] * chord_diff[:, source : source + 1]
    neighbours = plus_one + minus_one + cell_above + cell_below
    return diagonal[None] * adjoint - neighbours + transport + spectral_scale * spectral


def spectral_term(adjoint):
    positions = jnp.arange(NT, dtype=jnp.int32)
    full_weights = spectral_weights(positions[:, None] - positions[None, :])
    mixed_block = jnp.einsum(
        "st,skxy->tkxy",
        full_weights,
        lax.all_to_all(adjoint, "inst", split_axis=2, concat_axis=0, tiled=True),
        precision=lax.Precision.HIGHEST,
    )
    return lax.all_to_all(mixed_block, "inst", split_axis=0, concat_axis=2, tiled=True)


def body(
    start_adjoint,
    adjoint_source,
    diagonal,
    flux_x,
    flux_y,
    shape_derivative,
    mode_basis,
    patch_of_cell,
):
    adjoint = start_adjoint
    block_width = adjoint.shape[2]
    for repeat in range(SWEEPS):
        padded = with_halo(adjoint, (("space", 2),), 2)
        plus_one = padded[:, :, 3 : 3 + block_width]
        minus_one = padded[:, :, 1 : 1 + block_width]
        plus_two = padded[:, :, 4 : 4 + block_width]
        minus_two = padded[:, :, 0:block_width]
        spectral = spectral_term(adjoint)
        operated = apply_operator(
            adjoint, plus_one, minus_one, plus_two, minus_two, spectral, diagonal, flux_x, flux_y
        )
        adjoint = adjoint + (adjoint_source - operated) / diagonal[None]
    weight_sum = jnp.sum(adjoint * shape_derivative, axis=(0, 1))
    owners = patch_of_cell.reshape(1, -1)
    weighted = (mode_basis * weight_sum[:, :, None]).reshape(-1, mode_basis.shape[2])
    patch_ids = jnp.arange(PATCH_DEV * lax.axis_size(("inst", "space")), dtype=jnp.int32)
    onehot = (patch_ids[:, None] == owners).astype(jnp.float32)
    sensitivity = lax.psum_scatter(
        jnp.dot(
            onehot, weighted, precision=lax.Precision.HIGHEST, preferred_element_type=jnp.float32
        ),
        ("inst", "space"),
        scatter_dimension=0,
        tiled=True,
    )
    return (adjoint, sensitivity)


def solution(mesh):
    placed = (
        P("inst", None, "space", None),
        P("inst", None, "space", None),
        P(None, "space", None),
        P("inst", None, None, "space", None),
        P("inst", None, None, "space", None),
        P("inst", None, "space", None),
        P("space", None, None),
        P("space", None),
    )
    return jax.shard_map(
        body,
        mesh=mesh,
        in_specs=placed,
        out_specs=(P("inst", None, "space", None), P(("inst", "space"), None)),
        check_vma=False,
    )
```

profile of v0, /device:TPU:0, one launch (start us, length us, event | category | flops | bytes accessed | tf_op | source)
XLA Modules:
  0.0 246.4 jit_solution(7589216632292446299)
XLA Ops:
  7.2 2.5 %copy.77 = f32[8,6,8,512]{3,0,1,2:T(8,128)} copy(f32[8,6,8,512]{3,2,1,0:T(8,128)} %param.8) | data formatting | bytes 1572864 | tf_op args[0]
  9.7 5.2 %all-to-all-start = ((f32[8,6,8,512]{3,0,1,2:T(8,128)}), f32[8,6,8,512]{3,0,1,2:T(8,128)S(1)}, u32[]{:S(2)}, u32[]{:S(2)}) async-start(f32[8,6,8,512]{3,0,1,2:T(8,128)} %copy.77), calls=%async_computation | async-start | bytes 1572864 | tf_op jit(solution)/shard_map/all_to_all | solution.py:59
  15.9 3.5 %collective-permute-start = (f32[8,6,2,512]{3,0,2,1:T(8,128)}, f32[8,6,2,512]{3,0,2,1:T(8,128)}, u32[]{:S(2)}, u32[]{:S(2)}) collective-permute-start(f32[8,6,2,512]{3,0,2,1:T(8,128)} %copy.181), channel_id=1, source_target_pairs={{1,0},{2,1},{3,2},{4,3},{5,4},{6,5},{7,6},{0,7},{9,8},{10,9},{11,1... | collective-permute-start | bytes 589832 | tf_op jit(solution)/shard_map/ppermute | solution.py:23
  19.4 7.2 %fusion.85 = (f32[8,1,6,8,512]{4,3,2,1,0:T(8,128)S(1)}, f32[8,1,6,8,512]{4,3,2,1,0:T(8,128)}, f32[8,1,6,8,512]{4,3,2,1,0:T(8,128)}, f32[8,1,6,8,512]{4,3,2,1,0:T...) fusion(f32[8,6,6,8,512]{4,3,2,1,0:T(8,128)} %param.12, ...), kind=kLoop, calls=%fused_computation.152 | loop fusion | bytes 18874368 | tf_op jit(solution)/shard_map/slice | solution.py:48
  27.9 1.1 fusion.19
  29.7 1.4 constant_dynamic-update-slice_fusion.1
  32.0 1.5 copy.79
  33.5 4.2 %all-to-all-start.1 = ((f32[32,6,2,512]{3,2,1,0:T(2,128)}), f32[32,6,2,512]{3,2,1,0:T(2,128)S(1)}, u32[]{:S(2)}, u32[]{:S(2)}) async-start(f32[32,6,2,512]{3,2,1,0:T(2,128)} %copy.79), calls=%async_computation.1 | async-start | bytes 1572864 | tf_op jit(solution)/shard_map/all_to_all | solution.py:62
  38.6 1.7 fusion.8
  41.3 5.6 %all-to-all-done.1 = f32[32,6,2,512]{3,2,1,0:T(2,128)S(1)} async-done(((f32[32,6,2,512]{3,2,1,0:T(2,128)}), f32[32,6,2,512]{3,2,1,0:T(2,128)S(1)}, u32[]{:S(2)}, u32[]{:S(2)}) %all-to-all-start.1) | async-done | bytes 786464 | tf_op jit(solution)/shard_map/all_to_all | solution.py:62
  48.3 15.1 %divide_add_fusion.1 = f32[8,6,8,512]{3,0,2,1:T(8,128)S(1)} fusion(f32[8,6,8,512]{3,0,2,1:T(8,128)S(1)} %bitcast.164, f32[8,1,6,8,512]{4,3,2,1,0:T(8,128)} %get-tuple-element.54, f32[8,1,6,8,512]{4,3,2,1,0:T(8,128)} %get-tuple-element.13, f32[8,1,6,8,512]{4,3,2,1,0:T(8,128)} %get-tuple-element.55, f32[8,1,6,8,512]{4,3,2,1,0:T(8,128)} %get-tuple-element.12, ...), kind=kLoop, calls=%fused_computation.39 | loop fusion | flops 6488064 | bytes 17396736 | tf_op jit(solution)/shard_map/add | solution.py:87
  64.4 3.5 %all-to-all-start.2 = ((f32[8,6,8,512]{3,0,1,2:T(8,128)}), f32[8,6,8,512]{3,0,1,2:T(8,128)S(1)}, u32[]{:S(2)}, u32[]{:S(2)}) async-start(f32[8,6,8,512]{3,0,1,2:T(8,128)} %copy.83), calls=%async_computation.2 | async-start | bytes 1572864 | tf_op jit(solution)/shard_map/all_to_all | solution.py:59
  68.0 3.5 %collective-permute-start.2 = (f32[8,6,2,512]{3,0,2,1:T(8,128)S(1)}, f32[8,6,2,512]{3,0,2,1:T(8,128)S(1)}, u32[]{:S(2)}, u32[]{:S(2)}) collective-permute-start(f32[8,6,2,512]{3,0,2,1:T(8,128)S(1)} %get-tuple-element.38), channel_id=1, source_target_pairs={{1,0},{2,1},{3,2},{4,3},{5,4},{6,5},{7,6},{0,7},{9,8},{10,9},{11,1... | collective-permute-start | bytes 589832 | tf_op jit(solution)/shard_map/ppermute | solution.py:23
  71.5 6.7 %all-to-all-done.2 = f32[8,6,8,512]{3,0,1,2:T(8,128)S(1)} async-done(((f32[8,6,8,512]{3,0,1,2:T(8,128)}), f32[8,6,8,512]{3,0,1,2:T(8,128)S(1)}, u32[]{:S(2)}, u32[]{:S(2)}) %all-to-all-start.2) | async-done | bytes 786464 | tf_op jit(solution)/shard_map/all_to_all | solution.py:59
  79.1 1.5 copy.85
  80.6 4.2 %all-to-all-start.3 = ((f32[32,6,2,512]{3,2,1,0:T(2,128)}), f32[32,6,2,512]{3,2,1,0:T(2,128)}, u32[]{:S(2)}, u32[]{:S(2)}) async-start(f32[32,6,2,512]{3,2,1,0:T(2,128)} %copy.85), calls=%async_computation.3 | async-start | bytes 1572864 | tf_op jit(solution)/shard_map/all_to_all | solution.py:62
  86.3 1.1 fusion.29
  88.6 6.6 %all-to-all-done.3 = f32[32,6,2,512]{3,2,1,0:T(2,128)} async-done(((f32[32,6,2,512]{3,2,1,0:T(2,128)}), f32[32,6,2,512]{3,2,1,0:T(2,128)}, u32[]{:S(2)}, u32[]{:S(2)}) %all-to-all-start.3) | async-done | bytes 786464 | tf_op jit(solution)/shard_map/all_to_all | solution.py:62
  95.2 1.7 broadcast_multiply_fusion.1
  97.3 13.5 %fusion.13 = (f32[8,512]{1,0:T(8,128)S(1)}, f32[8,6,8,512]{3,0,2,1:T(8,128)}) fusion(f32[8,6,8,512]{3,2,1,0:T(8,128)} %param.13, f32[8,6,8,512]{3,0,2,1:T(8,128)S(1)} %divide_add_fusion.1, f32[8,6,8,512]{3,0,2,1:T(8,128)S(1)} %bitcast.163, f32[8,8,512]{2,0,1:T(8,128)} %get-tuple-element.25, f32[8,1,6,8,512]{4,3,2,1,0:T(8,128)S(1)} %get-tuple-element.8, ...), kind=kLoop, calls=%fused_computation.35 | loop fusion | flops 7270400 | bytes 17019904 | tf_op jit(solution)/shard_map/reduce_sum | solution.py:88
  111.4 3.0 %fusion = f32[256,128]{1,0:T(8,128)} fusion(f32[4096,128]{1,0:T(8,128)S(1)} %bitcast.162, s32[4096]{0:T(1024)S(1)} %bitcast.169), kind=kOutput, calls=%fused_computation.1 | convolution fusion | flops 1611661312 | bytes 2244608 | tf_op jit(solution)/shard_map/dot_general | solution.py:94
  114.4 1.3 copy.89
  115.8 122.5 %all-reduce.7.cloned.1.call-done = f32[256,128]{1,0:T(8,128)} async-done(((f32[256,128]{1,0:T(8,128)}), f32[256,128]{1,0:T(8,128)}) %all-reduce.7.cloned.1.call-update) | async-done | bytes 131088
  238.3 1.3 constant_dynamic-slice_fusion
  (82 shorter events, 12.5 us)
Async XLA Ops:
  7.2 7.7 %copy-start = (f32[8,6,8,512]{3,2,1,0:T(8,128)S(1)}, f32[8,6,8,512]{3,2,1,0:T(8,128)}, u32[]{:S(2)}) copy-start(f32[8,6,8,512]{3,2,1,0:T(8,128)} %param.8) | copy-start | bytes 2359300
  9.7 21.4 %all-to-all-start = ((f32[8,6,8,512]{3,0,1,2:T(8,128)}), f32[8,6,8,512]{3,0,1,2:T(8,128)S(1)}, u32[]{:S(2)}, u32[]{:S(2)}) async-start(f32[8,6,8,512]{3,0,1,2:T(8,128)} %copy.77), calls=%async_computation | async-start | bytes 1572864 | tf_op jit(solution)/shard_map/all_to_all | solution.py:59
  15.1 13.9 %collective-permute-start.1 = (f32[8,6,2,512]{3,0,2,1:T(8,128)S(1)}, f32[8,6,2,512]{3,0,2,1:T(8,128)S(1)}, u32[]{:S(2)}, u32[]{:S(2)}) collective-permute-start(f32[8,6,2,512]{3,0,2,1:T(8,128)S(1)} %copy.180), channel_id=1, source_target_pairs={{0,1},{1,2},{2,3},{3,4},{4,5},{5,6},{6,7},{7,0},{8,9},{9,10},{10,1... | collective-permute-start | bytes 589832 | tf_op jit(solution)/shard_map/ppermute | solution.py:21
  15.9 21.8 %collective-permute-start = (f32[8,6,2,512]{3,0,2,1:T(8,128)}, f32[8,6,2,512]{3,0,2,1:T(8,128)}, u32[]{:S(2)}, u32[]{:S(2)}) collective-permute-start(f32[8,6,2,512]{3,0,2,1:T(8,128)} %copy.181), channel_id=1, source_target_pairs={{1,0},{2,1},{3,2},{4,3},{5,4},{6,5},{7,6},{0,7},{9,8},{10,9},{11,1... | collective-permute-start | bytes 589832 | tf_op jit(solution)/shard_map/ppermute | solution.py:23
  27.4 2.3 copy-start.7
  33.5 13.4 %all-to-all-start.1 = ((f32[32,6,2,512]{3,2,1,0:T(2,128)}), f32[32,6,2,512]{3,2,1,0:T(2,128)S(1)}, u32[]{:S(2)}, u32[]{:S(2)}) async-start(f32[32,6,2,512]{3,2,1,0:T(2,128)} %copy.79), calls=%async_computation.1 | async-start | bytes 1572864 | tf_op jit(solution)/shard_map/all_to_all | solution.py:62
  46.9 1.3 copy-start.22
  46.9 1.3 copy-start.23
  46.9 1.4 copy-start.24
  63.4 4.5 %copy-start.25 = (s32[8,512]{1,0:T(8,128)S(1)}, s32[8,512]{1,0:T(8,128)}, u32[]{:S(2)}) copy-start(s32[8,512]{1,0:T(8,128)} %param.15) | copy-start | bytes 49156
  64.4 13.8 %all-to-all-start.2 = ((f32[8,6,8,512]{3,0,1,2:T(8,128)}), f32[8,6,8,512]{3,0,1,2:T(8,128)S(1)}, u32[]{:S(2)}, u32[]{:S(2)}) async-start(f32[8,6,8,512]{3,0,1,2:T(8,128)} %copy.83), calls=%async_computation.2 | async-start | bytes 1572864 | tf_op jit(solution)/shard_map/all_to_all | solution.py:59
  67.9 19.5 %collective-permute-start.3 = (f32[8,6,2,512]{3,0,2,1:T(8,128)S(1)}, f32[8,6,2,512]{3,0,2,1:T(8,128)S(1)}, u32[]{:S(2)}, u32[]{:S(2)}) collective-permute-start(f32[8,6,2,512]{3,0,2,1:T(8,128)S(1)} %get-tuple-element.39), channel_id=1, source_target_pairs={{0,1},{1,2},{2,3},{3,4},{4,5},{5,6},{6,7},{7,0},{8,9},{9,10},{10,1... | collective-permute-start | bytes 589832 | tf_op jit(solution)/shard_map/ppermute | solution.py:21
  68.0 19.4 %collective-permute-start.2 = (f32[8,6,2,512]{3,0,2,1:T(8,128)S(1)}, f32[8,6,2,512]{3,0,2,1:T(8,128)S(1)}, u32[]{:S(2)}, u32[]{:S(2)}) collective-permute-start(f32[8,6,2,512]{3,0,2,1:T(8,128)S(1)} %get-tuple-element.38), channel_id=1, source_target_pairs={{1,0},{2,1},{3,2},{4,3},{5,4},{6,5},{7,6},{0,7},{9,8},{10,9},{11,1... | collective-permute-start | bytes 589832 | tf_op jit(solution)/shard_map/ppermute | solution.py:23
  80.6 14.6 %all-to-all-start.3 = ((f32[32,6,2,512]{3,2,1,0:T(2,128)}), f32[32,6,2,512]{3,2,1,0:T(2,128)}, u32[]{:S(2)}, u32[]{:S(2)}) async-start(f32[32,6,2,512]{3,2,1,0:T(2,128)} %copy.85), calls=%async_computation.3 | async-start | bytes 1572864 | tf_op jit(solution)/shard_map/all_to_all | solution.py:62
  84.8 153.5 %all-reduce.7.cloned.1.call-start = ((), (), s32[]{:S(2)}) async-start(), calls=%async_computation.4 | async-start | bytes 262144
  85.4 2.0 copy-start.9
  87.6 9.6 %copy-start.1 = (f32[8,1,6,8,512]{4,3,2,1,0:T(8,128)S(1)}, f32[8,1,6,8,512]{4,3,2,1,0:T(8,128)}, u32[]{:S(2)}) copy-start(f32[8,1,6,8,512]{4,3,2,1,0:T(8,128)} %get-tuple-element.9) | copy-start | bytes 2359300
  87.6 9.6 %copy-start.2 = (f32[8,1,6,8,512]{4,3,2,1,0:T(8,128)S(1)}, f32[8,1,6,8,512]{4,3,2,1,0:T(8,128)}, u32[]{:S(2)}) copy-start(f32[8,1,6,8,512]{4,3,2,1,0:T(8,128)} %get-tuple-element.10) | copy-start | bytes 2359300
  95.2 2.0 copy-start.3
  95.2 2.0 copy-start.4
  95.2 2.0 copy-start.5
  95.2 2.1 copy-start.6
  97.3 13.5 %copy-start.12 = (f32[8,512,128]{2,1,0:T(8,128)S(1)}, f32[8,512,128]{2,1,0:T(8,128)}, u32[]{:S(2)}) copy-start(f32[8,512,128]{2,1,0:T(8,128)} %param.14) | copy-start | bytes 6291460
  111.4 3.0 %copy-start.11 = (f32[8,6,8,512]{3,0,2,1:T(8,128)S(1)}, f32[8,6,8,512]{3,0,2,1:T(8,128)}, u32[]{:S(2)}) copy-start(f32[8,6,8,512]{3,0,2,1:T(8,128)} %get-tuple-element.7) | copy-start | bytes 2359300
  (11 other events, 12.1 us)
Sparse Core Ops, SparseCore 0:
  114.5 123.6 all-reduce.6
where the time goes:
time: 247 us; the launch traced here: 246 us
  waiting for transfers between devices  141 us (57%)
  other arithmetic  35.4 us (14%)
  local copies, waits for them, and re-layouts  25.9 us (10%)
  starting transfers between devices  24.5 us (10%)
  between operations  14.4 us (6%)
  matrix products  4.71 us (2%)
    unnamed x2, waiting for transfers between devices  123 us
    add x1, other arithmetic, body(): adjoint = adjoint + (adjoint_source - operated) / diagonal[None]  15.1 us
    reduce_sum x1, other arithmetic, body(): weight_sum = jnp.sum(adjoint * shape_derivative, axis=(0, 1))  13.5 us
    all_to_all x2, waiting for transfers between devices, spectral_term(): lax.all_to_all(mixed_block, 'inst', split_axis=0, concat_axis=2, tiled=True)  12.2 us
    unnamed x62, local copies, waits for them, and re-layouts  10.6 us
    all_to_all x2, starting transfers between devices, spectral_term(): lax.all_to_all(adjoint, 'inst', split_axis=2, concat_axis=0, tiled=True)  8.69 us
    all_to_all x2, starting transfers between devices, spectral_term(): lax.all_to_all(mixed_block, 'inst', split_axis=0, concat_axis=2, tiled=True)  8.4 us
    slice x1, local copies, waits for them, and re-layouts, apply_operator(): transport = transport + flux_y[:, source] * chord_diff[:, source:source + 1]  7.25 us
  transfers between devices with their start and end apart: 9, of which 4 were waited for; matrix products, arithmetic and copies ran while one was open for 10% of the time, Pallas kernels for 0%

commit v1 on v0

v1 whole, which is shorter than its diff:
```python
import math

import jax
import jax.numpy as jnp
import numpy as np
from jax import lax
from jax.experimental import pallas as pl
from jax.experimental.pallas import tpu as pltpu
from jax.sharding import PartitionSpec as P

NT = 32
PATCH_DEV = 8
REACH = 16
LANES = 128
SCALE = 0.1
F32 = jnp.float32


def weight_matrix(count):
    weights = np.zeros((count, count))
    for s in range(count):
        for t in range(count):
            if s != t:
                angle = math.pi * (s - t) / count
                weights[s, t] = 0.5 * (-1.0) ** (s - t) * math.cos(angle) / math.sin(angle)
    return weights


def circulant_apply(values):
    count = len(values)
    row = weight_matrix(count)[:, 0]
    if count == 2:
        return None
    half = count // 2
    total = [values[s] + values[s + half] for s in range(half)]
    diff = [values[s] - values[s + half] for s in range(half)]
    even = circulant_apply(total)
    q = [(row[d] - row[d + half]) / 2 for d in range(half)]
    quarter = half // 2

    def at(position):
        position %= count
        return (diff[position], 1.0) if position < half else (diff[position - half], -1.0)

    out = [None] * count
    for t in range(half):
        acc = None
        for d in range(1, quarter):
            plus, sign_plus = at(t + d)
            minus, sign_minus = at(t - d)
            pair = plus - minus if sign_plus == sign_minus else plus + minus
            term = float(q[d] * sign_plus) * pair
            acc = term if acc is None else acc + term
        last, sign = at(t + quarter)
        term = float(q[quarter] * sign) * last
        acc = term if acc is None else acc + term
        if even is None:
            out[t], out[t + half] = acc, -acc
        else:
            out[t], out[t + half] = even[t] + acc, even[t] - acc
    return out


def chunk_place(chunk, n_inst, ny):
    split = n_inst // (ny // LANES)
    return chunk // split, chunk % split


def lane_tile(index):
    return pl.ds(pl.multiple_of(index * LANES, LANES), LANES)


def pack_rows(row_block, first_row, ny):
    tiles = ny // LANES
    sub = lax.broadcasted_iota(jnp.int32, (8, LANES), 0)
    packed = None
    for y in range(tiles):
        tile = row_block[:, y * LANES : (y + 1) * LANES]
        shift = (2 * y - first_row) % 8
        moved = pltpu.roll(tile, shift, 0) if shift else tile
        packed = moved if packed is None else jnp.where(sub >= 2 * y, moved, packed)
    return packed


def pack_kernel(n_inst, a_ref, *refs):
    chunks, (first_ref, last_ref) = refs[:n_inst], refs[n_inst:]
    steps, nv, _, ny = a_ref.shape
    split = n_inst // (ny // LANES)
    part = nv // split
    me = lax.axis_index("inst")

    def at_step(t, _):
        for r in range(n_inst):
            y, v = chunk_place(me ^ r, n_inst, ny)
            for k in range(part):
                chunks[r][t, k] = a_ref[t, v * part + k, :, lane_tile(y)]
        for k in range(nv):
            rows = a_ref[t, k]
            first_ref[t, k] = pack_rows(rows, 0, ny)
            last_ref[t, k] = pack_rows(rows, 6, ny)
        return 0

    lax.fori_loop(0, steps, at_step, 0)


def local_terms(a_ref, prev_ref, next_ref, pitch, chord, near):
    nv, rows, ny = pitch.shape
    tiles = ny // LANES
    sub = lax.broadcasted_iota(jnp.int32, (rows, ny), 0)
    lane = lax.broadcasted_iota(jnp.int32, (rows, ny), 1)
    for k in range(nv):
        a = a_ref[0, k]
        before, after = prev_ref[0, k], next_ref[0, k]
        low = jnp.concatenate(
            [pltpu.roll(before, (-2 * y) % 8, 0) if y else before for y in range(tiles)], axis=1
        )
        high = jnp.concatenate(
            [pltpu.roll(after, 6 - 2 * y, 0) if y != 3 else after for y in range(tiles)], axis=1
        )
        edge = jnp.where(sub < 4, low, high)
        plus_two = jnp.where(sub >= 6, edge, pltpu.roll(a, 6, 0))
        plus_one = jnp.where(sub == 7, pltpu.roll(edge, 1, 0), pltpu.roll(a, 7, 0))
        minus_two = jnp.where(sub < 2, edge, pltpu.roll(a, 2, 0))
        minus_one = jnp.where(sub == 0, pltpu.roll(edge, 7, 0), pltpu.roll(a, 1, 0))
        above = jnp.where(lane == ny - 1, 0.0, pltpu.roll(a, ny - 1, 1))
        below = jnp.where(lane == 0, 0.0, pltpu.roll(a, 1, 1))
        pitch[k] = 2.0 / 3.0 * (plus_one - minus_one) - 1.0 / 12.0 * (plus_two - minus_two)
        chord[k] = above - below
        near[k] = plus_one + minus_one + above + below


def fresh_tile(k, y, src_ref, fx_ref, fy_ref, pitch_tiles, chord_tiles, near, inverse):
    lanes = slice(y * LANES, (y + 1) * LANES)
    acc = src_ref[0, k, :, lanes] + near[k, :, lanes]
    for j in range(len(pitch_tiles)):
        acc = acc - fx_ref[0, j, k, :, lanes] * pitch_tiles[j]
        acc = acc - fy_ref[0, j, k, :, lanes] * chord_tiles[j]
    return acc * inverse[k, :, lanes]


def first_sweep_kernel(
    n_inst, a_ref, prev_ref, next_ref, src_ref, d_ref, fx_ref, fy_ref, *refs
):
    out_refs, (whole, pitch, chord, near, inverse) = refs[:n_inst], refs[n_inst:]
    nv, _, ny = pitch.shape
    part = out_refs[0].shape[1]
    me = lax.axis_index("inst")

    @pl.when(pl.program_id(0) == 0)
    def _():
        inverse[...] = 1.0 / d_ref[...]

    local_terms(a_ref, prev_ref, next_ref, pitch, chord, near)
    for y in range(ny // LANES):
        lanes = slice(y * LANES, (y + 1) * LANES)
        pitch_tiles = [pitch[j, :, lanes] for j in range(nv)]
        chord_tiles = [chord[j, :, lanes] for j in range(nv)]
        for k in range(nv):
            whole[y * nv + k] = fresh_tile(
                k, y, src_ref, fx_ref, fy_ref, pitch_tiles, chord_tiles, near, inverse
            )
    for r in range(n_inst):
        base = (me ^ r) * part
        for k in range(part):
            out_refs[r][0, k] = whole[base + k]


def spectral_kernel(n_inst, second, d_ref, *refs):
    in_refs = refs[:n_inst]
    shift_refs = refs[n_inst : 2 * n_inst] if second else ()
    out_refs = refs[(2 if second else 1) * n_inst : (3 if second else 2) * n_inst]
    (work,) = refs[(3 if second else 2) * n_inst :]
    per, part = in_refs[0].shape[:2]
    ny = d_ref.shape[2]
    me = lax.axis_index("inst")
    y, v = chunk_place(me, n_inst, ny)

    def at_tile(c, _):
        for r in range(n_inst):
            base = (me ^ r) * per
            for t in range(per):
                value = in_refs[r][t, c]
                if second:
                    value = value - shift_refs[r][t, c]
                work[base + t] = value
        out = circulant_apply([work[s] for s in range(NT)])
        factor = SCALE / d_ref[v * part + c, :, lane_tile(y)]
        for s in range(NT):
            work[s] = out[s] * factor
        for r in range(n_inst):
            base = (me ^ r) * per
            for t in range(per):
                out_refs[r][t, c] = work[base + t]
        return 0

    lax.fori_loop(0, part, at_tile, 0)


def join_kernel(n_inst, *refs):
    b_refs, z_refs = refs[:n_inst], refs[n_inst : 2 * n_inst]
    a_ref, first_ref, last_ref = refs[2 * n_inst :]
    steps, nv, _, ny = a_ref.shape
    part = b_refs[0].shape[1]
    me = lax.axis_index("inst")

    def at_step(t, _):
        for r in range(n_inst):
            y, v = chunk_place(me ^ r, n_inst, ny)
            for k in range(part):
                a_ref[t, v * part + k, :, lane_tile(y)] = b_refs[r][t, k] - z_refs[r][t, k]
        for k in range(nv):
            rows = a_ref[t, k]
            first_ref[t, k] = pack_rows(rows, 0, ny)
            last_ref[t, k] = pack_rows(rows, 6, ny)
        return 0

    lax.fori_loop(0, steps, at_step, 0)


def second_sweep_kernel(
    a_ref, prev_ref, next_ref, src_ref, d_ref, fx_ref, fy_ref, shape_ref, out_ref, weight_ref,
    pitch, chord, near, inverse,
):
    nv, _, ny = pitch.shape

    @pl.when(pl.program_id(0) == 0)
    def _():
        inverse[...] = 1.0 / d_ref[...]
        weight_ref[...] = jnp.zeros_like(weight_ref)

    local_terms(a_ref, prev_ref, next_ref, pitch, chord, near)
    for y in range(ny // LANES):
        lanes = slice(y * LANES, (y + 1) * LANES)
        pitch_tiles = [pitch[j, :, lanes] for j in range(nv)]
        chord_tiles = [chord[j, :, lanes] for j in range(nv)]
        weight = weight_ref[:, lanes]
        for k in range(nv):
            value = fresh_tile(
                k, y, src_ref, fx_ref, fy_ref, pitch_tiles, chord_tiles, near, inverse
            )
            out_ref[0, k, :, lanes] = value
            weight = weight + value * shape_ref[0, k, :, lanes]
        weight_ref[:, lanes] = weight


def last_kernel(n_inst, x_ref, weight_ref, shape_ref, mode_ref, patch_ref, *refs):
    z_refs, (a_ref, send_ref, weight) = refs[:n_inst], refs[n_inst:]
    steps, nv, rows, ny = x_ref.shape
    part = z_refs[0].shape[1]
    me, space = lax.axis_index("inst"), lax.axis_index("space")
    owners = send_ref.shape[0]
    per_space = PATCH_DEV * n_inst
    window = per_space + 2 * REACH
    weight[...] = weight_ref[...]

    def at_step(t, _):
        for r in range(n_inst):
            y, v = chunk_place(me ^ r, n_inst, ny)
            total = jnp.zeros((rows, LANES), F32)
            for k in range(part):
                z = z_refs[r][t, k]
                a_ref[t, v * part + k, :, lane_tile(y)] = (
                    x_ref[t, v * part + k, :, lane_tile(y)] - z
                )
                total = total + z * shape_ref[t, v * part + k, :, lane_tile(y)]
            weight[:, lane_tile(y)] = weight[:, lane_tile(y)] - total
        return 0

    lax.fori_loop(0, steps, at_step, 0)
    first = per_space * space - REACH
    ids = lax.broadcasted_iota(jnp.int32, (window, ny), 0) + first
    acc = jnp.zeros((window, LANES), F32)
    for x in range(rows):
        hit = jnp.where(ids == patch_ref[x : x + 1, :], weight[x : x + 1, :], 0.0)
        acc = acc + jnp.dot(
            hit, mode_ref[x], precision=lax.Precision.HIGHEST, preferred_element_type=F32
        )
    send_ref[...] = jnp.zeros_like(send_ref)
    first_owner = n_inst * space - REACH // PATCH_DEV
    for j in range(window // PATCH_DEV):
        owner = first_owner + j

        @pl.when((owner >= 0) & (owner < owners))
        def _():
            send_ref[owner] = acc[j * PATCH_DEV : (j + 1) * PATCH_DEV]


def call(kernel, outs, scratch=(), **kwargs):
    return pl.pallas_call(
        kernel,
        out_shape=[jax.ShapeDtypeStruct(shape, F32) for shape in outs],
        scratch_shapes=[pltpu.VMEM(shape, F32) for shape in scratch],
        **kwargs,
    )


def make_body(n_inst, n_space):
    def exchange(chunks):
        return [chunks[0]] + [
            lax.ppermute(chunks[r], "inst", [(i, i ^ r) for i in range(n_inst)])
            for r in range(1, n_inst)
        ]

    def edges(first, last):
        ring = [(i, (i + 1) % n_space) for i in range(n_space)]
        before = lax.ppermute(last, "space", ring)
        after = lax.ppermute(first, "space", [(j, i) for i, j in ring])
        return before, after

    def body(start, source, diagonal, flux_x, flux_y, shape_derivative, mode_basis, patch_of_cell):
        steps, nv, rows, ny = start.shape
        part = nv * (ny // LANES) // n_inst
        chunk = (steps, part, 8, LANES)
        edge = (steps, nv, 8, LANES)
        tile = (nv, rows, ny)

        def per_step(shape):
            return pl.BlockSpec((1,) + shape[1:], lambda t: (t,) + (0,) * (len(shape) - 1))

        def fixed(shape):
            return pl.BlockSpec(shape, lambda t: (0,) * len(shape))

        def bound(kernel, *args):
            def run(*refs):
                kernel(*args, *refs)

            return run

        sweep_specs = [
            per_step(start.shape), per_step(edge), per_step(edge), per_step(source.shape),
            fixed(diagonal.shape), per_step(flux_x.shape), per_step(flux_y.shape),
        ]

        *chunks, first, last = call(
            bound(pack_kernel, n_inst), [chunk] * n_inst + [edge] * 2, name="pack"
        )(start)
        start_cells = exchange(chunks)
        before, after = edges(first, last)
        b = call(
            bound(first_sweep_kernel, n_inst), [chunk] * n_inst,
            scratch=[(nv * ny // LANES, 8, LANES), tile, tile, tile, tile],
            grid=(steps,), in_specs=sweep_specs, out_specs=[per_step(chunk)] * n_inst,
            name="sweep1",
        )(start, before, after, source, diagonal, flux_x, flux_y)
        b_cells = exchange(b)
        z0_cells = call(
            bound(spectral_kernel, n_inst, False), [chunk] * n_inst, scratch=[(NT, 8, LANES)],
            name="spectral1",
        )(diagonal, *start_cells)
        z0 = exchange(z0_cells)
        z1_cells = call(
            bound(spectral_kernel, n_inst, True), [chunk] * n_inst, scratch=[(NT, 8, LANES)],
            name="spectral2",
        )(diagonal, *b_cells, *z0_cells)
        z1 = exchange(z1_cells)
        a1, first, last = call(
            bound(join_kernel, n_inst), [start.shape, edge, edge], name="join"
        )(*b, *z0)
        before, after = edges(first, last)
        x, weight = call(
            second_sweep_kernel, [start.shape, (rows, ny)], scratch=[tile] * 4,
            grid=(steps,), in_specs=sweep_specs + [per_step(shape_derivative.shape)],
            out_specs=[per_step(start.shape), fixed((rows, ny))],
            name="sweep2",
        )(a1, before, after, source, diagonal, flux_x, flux_y, shape_derivative)
        owners = n_inst * n_space
        adjoint, sends = call(
            bound(last_kernel, n_inst), [start.shape, (owners, PATCH_DEV, LANES)],
            scratch=[(rows, ny)], name="last",
        )(x, weight, shape_derivative, mode_basis, patch_of_cell, *z1)
        parts = lax.all_to_all(sends, ("inst", "space"), 0, 0, tiled=True)
        return adjoint, jnp.sum(parts, axis=0)

    return body


def solution(mesh):
    placed = (
        P("inst", None, "space", None),
        P("inst", None, "space", None),
        P(None, "space", None),
        P("inst", None, None, "space", None),
        P("inst", None, None, "space", None),
        P("inst", None, "space", None),
        P("space", None, None),
        P("space", None),
    )
    return jax.shard_map(
        make_body(mesh.shape["inst"], mesh.shape["space"]),
        mesh=mesh,
        in_specs=placed,
        out_specs=(P("inst", None, "space", None), P(("inst", "space"), None)),
        check_vma=False,
    )
```

time: 247 us -> 80.6 us (0.33)
  waiting for transfers between devices: 141 us -> 5.75 us
  other arithmetic: 35.4 us -> 0.63 us
  Pallas kernels: 0 us -> 31.9 us
  local copies, waits for them, and re-layouts: 25.9 us -> 5.87 us
  between operations: 14.4 us -> 0.76 us
  blocking collectives: 0 us -> 13 us
  matrix products: 4.71 us -> 0 us
    unnamed x2 -> x0, waiting for transfers between devices: 123 us -> none
    pallas_call x0 -> x7, Pallas kernels: none -> 31.9 us  [the longest x1 8.19 us: body(): call(second_sweep_kernel, [start.shape, (rows, ny)], scratch=[tile] * 4,...]
    all_to_all x4 -> x0, waiting for transfers between devices: 18.9 us -> none  [the longest x2 12.2 us: spectral_term(): lax.all_to_all(mixed_block, 'inst', split_axis=0, concat_axis=2, tiled=True)]
    all_to_all x4 -> x0, starting transfers between devices: 17.1 us -> none  [the longest x2 8.69 us: spectral_term(): lax.all_to_all(adjoint, 'inst', split_axis=2, concat_axis=0, tiled=True)]
    add x1 -> x0, other arithmetic: 15.1 us -> none  [body(): adjoint = adjoint + (adjoint_source - operated) / diagonal[None]]
    ppermute x4 -> x16, starting transfers between devices: 7.18 us -> 22.1 us  [the longest x12 15 us: exchange(): lax.ppermute(chunks[r], 'inst', [(i, i ^ r) for i in range(n_inst)])]
    all_to_all x0 -> x1, blocking collectives: none -> 13 us  [body(): parts = lax.all_to_all(sends, ('inst', 'space'), 0, 0, tiled=True)]
    reduce_sum x1, other arithmetic: 13.5 us -> 0.63 us  [body(): return (adjoint, jnp.sum(parts, axis=0))]
  transfers between devices with their start and end apart: 9 -> 16, of which waited for: 4 -> 2; matrix products, arithmetic and copies ran while one was open for 10% -> 0% of each run, Pallas kernels for 0% -> 31%
where the time goes in v1:
time: 80.6 us; the launch traced here: 80 us
  Pallas kernels  31.9 us (40%)
  starting transfers between devices  22.1 us (27%)
  blocking collectives  13 us (16%)
  local copies, waits for them, and re-layouts  5.87 us (7%)
  waiting for transfers between devices  5.75 us (7%)
    ppermute x12, starting transfers between devices, exchange(): lax.ppermute(chunks[r], 'inst', [(i, i ^ r) for i in range(n_inst)])  15 us
    all_to_all x1, blocking collectives, body(): parts = lax.all_to_all(sends, ('inst', 'space'), 0, 0, tiled=True)  13 us
    pallas_call x1, Pallas kernels, body(): call(second_sweep_kernel, [start.shape, (rows, ny)], scratch=[tile] * 4,...  8.19 us
    pallas_call x1, Pallas kernels, body(): call(bound(first_sweep_kernel, n_inst), [chunk] * n_inst, scratch=[(nv *...  8.11 us
    ppermute x2, starting transfers between devices, edges(): after = lax.ppermute(first, 'space', [(j, i) for i, j in ring])  7.08 us
    unnamed x32, local copies, waits for them, and re-layouts  5.87 us
    ppermute x12, waiting for transfers between devices, exchange(): lax.ppermute(chunks[r], 'inst', [(i, i ^ r) for i in range(n_inst)])  5.74 us
    pallas_call x1, Pallas kernels, body(): call(bound(last_kernel, n_inst), [start.shape, (owners, PATCH_DEV, LANES)...  4.72 us
  transfers between devices with their start and end apart: 16, of which 2 were waited for; matrix products, arithmetic and copies ran while one was open for 0% of the time, Pallas kernels for 31%

profile of v1, /device:TPU:0, one launch (start us, length us, event | category | flops | bytes accessed | tf_op | source)
XLA Modules:
  0.0 80.0 jit_solution(6975394760936052633)
XLA Ops:
  0.6 2.3 %pack.1 = (f32[8,6,8,128]{3,2,1,0:T(8,128)}, f32[8,6,8,128]{3,2,1,0:T(8,128)}, f32[8,6,8,128]{3,2,1,0:T(8,128)}, f32[8,6,8,128]{3,2,1,0:T(8,128)}, f32[8,6,8,128]{3,2,1,0:T(8,128)}, /*index=5*/f32[8,6,8,128]{3,2,1,0:T(8,128)}) custom-call(f32[8,6,8,512]{3,2,1,0:T(8,128)} %refs_0_.5), custom_call_target="tpu_custom_call" | custom-call | tf_op jit(solution)/shard_map/pack/pallas_call | solution.py:334
  3.0 3.0 %collective-permute-start.2 = (f32[8,6,8,128]{3,2,1,0:T(8,128)}, f32[8,6,8,128]{3,2,1,0:T(8,128)S(1)}, u32[]{:S(2)}, u32[]{:S(2)}) collective-permute-start(f32[8,6,8,128]{3,2,1,0:T(8,128)} %get-tuple-element.34), channel_id=1, source_target_pairs={{0,8},{8,0},{16,24},{24,16},{1,9},{9,1},{17,25},{25,17},{2,10},{10... | collective-permute-start | bytes 589832 | tf_op jit(solution)/shard_map/ppermute | solution.py:300
  5.9 1.5 %collective-permute-start.3 = (f32[8,6,8,128]{3,2,1,0:T(8,128)}, f32[8,6,8,128]{3,2,1,0:T(8,128)S(1)}, u32[]{:S(2)}, u32[]{:S(2)}) collective-permute-start(f32[8,6,8,128]{3,2,1,0:T(8,128)} %get-tuple-element.35), channel_id=1, source_target_pairs={{0,16},{8,24},{16,0},{24,8},{1,17},{9,25},{17,1},{25,9},{2,18},{10... | collective-permute-start | bytes 589832 | tf_op jit(solution)/shard_map/ppermute | solution.py:300
  7.5 3.5 %collective-permute-start.1 = (f32[8,6,8,128]{3,2,1,0:T(8,128)}, f32[8,6,8,128]{3,2,1,0:T(8,128)S(1)}, u32[]{:S(2)}, u32[]{:S(2)}) collective-permute-start(f32[8,6,8,128]{3,2,1,0:T(8,128)} %get-tuple-element.28), channel_id=1, source_target_pairs={{1,0},{2,1},{3,2},{4,3},{5,4},{6,5},{7,6},{0,7},{9,8},{10,9},{11,1... | collective-permute-start | bytes 589832 | tf_op jit(solution)/shard_map/ppermute | solution.py:307
  11.0 0.9 %collective-permute-done.2.refs_2_ = f32[8,6,8,128]{3,2,1,0:T(8,128)S(1)} collective-permute-done((f32[8,6,8,128]{3,2,1,0:T(8,128)}, f32[8,6,8,128]{3,2,1,0:T(8,128)S(1)}, u32[]{:S(2)}, u32[]{:S(2)}) %collective-permute-start.2) | collective-permute-done | bytes 196640 | tf_op jit(solution)/shard_map/ppermute | solution.py:300
  11.9 4.8 %collective-permute-done.3.refs_3_ = f32[8,6,8,128]{3,2,1,0:T(8,128)S(1)} collective-permute-done((f32[8,6,8,128]{3,2,1,0:T(8,128)}, f32[8,6,8,128]{3,2,1,0:T(8,128)S(1)}, u32[]{:S(2)}, u32[]{:S(2)}) %collective-permute-start.3) | collective-permute-done | bytes 196640 | tf_op jit(solution)/shard_map/ppermute | solution.py:300
  17.5 2.8 %spectral1.1 = (f32[8,6,8,128]{3,2,1,0:T(8,128)}, f32[8,6,8,128]{3,2,1,0:T(8,128)}, f32[8,6,8,128]{3,2,1,0:T(8,128)}, f32[8,6,8,128]{3,2,1,0:T(8,128)}) custom-call(f32[6,8,512]{2,1,0:T(8,128)} %refs_0_.7, f32[8,6,8,128]{3,2,1,0:T(8,128)} %get-tuple-element.33.refs_1_, f32[8,6,8,128]{3,2,1,0:T(8,128)} %copy-done.9, f32[8,6,8,128]{3,2,1,0:T(8,128)} %copy-done.10, ...), custom_call_target="tpu_custom_call" | custom-call | tf_op jit(solution)/shard_map/spectral1/pallas_call | solution.py:346
  20.3 1.2 %collective-permute-start.5 = (f32[8,6,8,128]{3,2,1,0:T(8,128)}, f32[8,6,8,128]{3,2,1,0:T(8,128)S(1)}, u32[]{:S(2)}, u32[]{:S(2)}) collective-permute-start(f32[8,6,8,128]{3,2,1,0:T(8,128)} %get-tuple-element.38.refs_6_), channel_id=1, source_target_pairs={{0,8},{8,0},{16,24},{24,16},{1,9},{9,1},{17,25},{25,17},{2,10},{10... | collective-permute-start | bytes 589832 | tf_op jit(solution)/shard_map/ppermute | solution.py:300
  21.5 0.9 %collective-permute-start.6 = (f32[8,6,8,128]{3,2,1,0:T(8,128)}, f32[8,6,8,128]{3,2,1,0:T(8,128)S(1)}, u32[]{:S(2)}, u32[]{:S(2)}) collective-permute-start(f32[8,6,8,128]{3,2,1,0:T(8,128)} %get-tuple-element.39.refs_7_), channel_id=1, source_target_pairs={{0,16},{8,24},{16,0},{24,8},{1,17},{9,25},{17,1},{25,9},{2,18},{10... | collective-permute-start | bytes 589832 | tf_op jit(solution)/shard_map/ppermute | solution.py:300
  22.4 1.4 %collective-permute-start.7 = (f32[8,6,8,128]{3,2,1,0:T(8,128)}, f32[8,6,8,128]{3,2,1,0:T(8,128)S(1)}, u32[]{:S(2)}, u32[]{:S(2)}) collective-permute-start(f32[8,6,8,128]{3,2,1,0:T(8,128)} %get-tuple-element.40.refs_8_), channel_id=1, source_target_pairs={{0,24},{8,16},{16,8},{24,0},{1,25},{9,17},{17,9},{25,1},{2,26},{10... | collective-permute-start | bytes 589832 | tf_op jit(solution)/shard_map/ppermute | solution.py:300
  25.2 8.1 %sweep1.1 = (f32[8,6,8,128]{3,2,1,0:T(8,128)}, f32[8,6,8,128]{3,2,1,0:T(8,128)}, f32[8,6,8,128]{3,2,1,0:T(8,128)}, f32[8,6,8,128]{3,2,1,0:T(8,128)}) custom-call(f32[8,6,8,512]{3,2,1,0:T(8,128)} %refs_0_.5, f32[8,6,8,128]{3,2,1,0:T(8,128)} %copy-done.13, f32[8,6,8,128]{3,2,1,0:T(8,128)} %copy-done.15, f32[8,6,8,512]{3,2,1,0:T(8,128)} %src_ref.1, ...), custom_call_target="tpu_custom_call" | custom-call | tf_op jit(solution)/shard_map/sweep1/pallas_call | solution.py:339
  33.3 1.2 %collective-permute-start.10 = (f32[8,6,8,128]{3,2,1,0:T(8,128)}, f32[8,6,8,128]{3,2,1,0:T(8,128)S(1)}, u32[]{:S(2)}, u32[]{:S(2)}) collective-permute-start(f32[8,6,8,128]{3,2,1,0:T(8,128)} %get-tuple-element.30.refs_1_), channel_id=1, source_target_pairs={{0,8},{8,0},{16,24},{24,16},{1,9},{9,1},{17,25},{25,17},{2,10},{10... | collective-permute-start | bytes 589832 | tf_op jit(solution)/shard_map/ppermute | solution.py:300
  34.5 1.0 %collective-permute-start.11 = (f32[8,6,8,128]{3,2,1,0:T(8,128)}, f32[8,6,8,128]{3,2,1,0:T(8,128)S(1)}, u32[]{:S(2)}, u32[]{:S(2)}) collective-permute-start(f32[8,6,8,128]{3,2,1,0:T(8,128)} %get-tuple-element.31.refs_2_), channel_id=1, source_target_pairs={{0,16},{8,24},{16,0},{24,8},{1,17},{9,25},{17,1},{25,9},{2,18},{10... | collective-permute-start | bytes 589832 | tf_op jit(solution)/shard_map/ppermute | solution.py:300
  35.4 1.4 %collective-permute-start.12 = (f32[8,6,8,128]{3,2,1,0:T(8,128)}, f32[8,6,8,128]{3,2,1,0:T(8,128)S(1)}, u32[]{:S(2)}, u32[]{:S(2)}) collective-permute-start(f32[8,6,8,128]{3,2,1,0:T(8,128)} %get-tuple-element.32.refs_3_), channel_id=1, source_target_pairs={{0,24},{8,16},{16,8},{24,0},{1,25},{9,17},{17,9},{25,1},{2,26},{10... | collective-permute-start | bytes 589832 | tf_op jit(solution)/shard_map/ppermute | solution.py:300
  37.6 2.6 %join.1 = (f32[8,6,8,512]{3,2,1,0:T(8,128)}, f32[8,6,8,128]{3,2,1,0:T(8,128)}, f32[8,6,8,128]{3,2,1,0:T(8,128)}) custom-call(f32[8,6,8,128]{3,2,1,0:T(8,128)} %get-tuple-element.29.refs_0_.refs_1_, f32[8,6,8,128]{3,2,1,0:T(8,128)} %get-tuple-element.30.refs_1_, f32[8,6,8,128]{3,2,1,0:T(8,128)} %get-tuple-element.31.refs_2_, ...), custom_call_target="tpu_custom_call" | custom-call | tf_op jit(solution)/shard_map/join/pallas_call | solution.py:356
  40.3 3.5 %collective-permute-start.9 = (f32[8,6,8,128]{3,2,1,0:T(8,128)}, f32[8,6,8,128]{3,2,1,0:T(8,128)S(1)}, u32[]{:S(2)}, u32[]{:S(2)}) collective-permute-start(f32[8,6,8,128]{3,2,1,0:T(8,128)} %get-tuple-element.43), channel_id=1, source_target_pairs={{1,0},{2,1},{3,2},{4,3},{5,4},{6,5},{7,6},{0,7},{9,8},{10,9},{11,1... | collective-permute-start | bytes 589832 | tf_op jit(solution)/shard_map/ppermute | solution.py:307
  44.6 0.7 copy-done.7
  45.3 3.1 %spectral2.1 = (f32[8,6,8,128]{3,2,1,0:T(8,128)}, f32[8,6,8,128]{3,2,1,0:T(8,128)}, f32[8,6,8,128]{3,2,1,0:T(8,128)}, f32[8,6,8,128]{3,2,1,0:T(8,128)}) custom-call(f32[6,8,512]{2,1,0:T(8,128)} %refs_0_.7, f32[8,6,8,128]{3,2,1,0:T(8,128)} %get-tuple-element.29.refs_0_.refs_1_, f32[8,6,8,128]{3,2,1,0:T(8,128)} %copy-done.3, f32[8,6,8,128]{3,2,1,0:T(8,128)} %copy-done.4, ...), custom_call_target="tpu_custom_call" | custom-call | tf_op jit(solution)/shard_map/spectral2/pallas_call | solution.py:351
  48.3 1.2 %collective-permute-start.13 = (f32[8,6,8,128]{3,2,1,0:T(8,128)}, f32[8,6,8,128]{3,2,1,0:T(8,128)S(1)}, u32[]{:S(2)}, u32[]{:S(2)}) collective-permute-start(f32[8,6,8,128]{3,2,1,0:T(8,128)} %get-tuple-element.47), channel_id=1, source_target_pairs={{0,8},{8,0},{16,24},{24,16},{1,9},{9,1},{17,25},{25,17},{2,10},{10... | collective-permute-start | bytes 589832 | tf_op jit(solution)/shard_map/ppermute | solution.py:300
  49.5 1.0 %collective-permute-start.14 = (f32[8,6,8,128]{3,2,1,0:T(8,128)}, f32[8,6,8,128]{3,2,1,0:T(8,128)S(1)}, u32[]{:S(2)}, u32[]{:S(2)}) collective-permute-start(f32[8,6,8,128]{3,2,1,0:T(8,128)} %get-tuple-element.48), channel_id=1, source_target_pairs={{0,16},{8,24},{16,0},{24,8},{1,17},{9,25},{17,1},{25,9},{2,18},{10... | collective-permute-start | bytes 589832 | tf_op jit(solution)/shard_map/ppermute | solution.py:300
  50.5 1.3 %collective-permute-start.15 = (f32[8,6,8,128]{3,2,1,0:T(8,128)}, f32[8,6,8,128]{3,2,1,0:T(8,128)S(1)}, u32[]{:S(2)}, u32[]{:S(2)}) collective-permute-start(f32[8,6,8,128]{3,2,1,0:T(8,128)} %get-tuple-element.49), channel_id=1, source_target_pairs={{0,24},{8,16},{16,8},{24,0},{1,25},{9,17},{17,9},{25,1},{2,26},{10... | collective-permute-start | bytes 589832 | tf_op jit(solution)/shard_map/ppermute | solution.py:300
  52.6 8.2 %sweep2.1 = (f32[8,6,8,512]{3,2,1,0:T(8,128)}, f32[8,512]{1,0:T(8,128)}) custom-call(f32[8,6,8,512]{3,2,1,0:T(8,128)} %get-tuple-element.41.a_ref, f32[8,6,8,128]{3,2,1,0:T(8,128)} %copy-done.12, f32[8,6,8,128]{3,2,1,0:T(8,128)} %copy-done.14, f32[8,6,8,512]{3,2,1,0:T(8,128)} %src_ref.1, f32[6,8,512]{2,1,0:T(8,128)} %refs_0_.7, f32[8,6,6,8,512]{4,3,2,1,0:T(8,128)} %fx_ref.1, ...), custom_call_target="tpu_custom_call" | custom-call | tf_op jit(solution)/shard_map/sweep2/pallas_call | solution.py:360
  61.6 4.7 %last.1 = (f32[8,6,8,512]{3,2,1,0:T(8,128)}, f32[32,8,128]{2,1,0:T(8,128)}) custom-call(f32[8,6,8,512]{3,2,1,0:T(8,128)} %get-tuple-element.44.refs_0_, f32[8,512]{1,0:T(8,128)} %get-tuple-element.45.refs_1_, f32[8,6,8,512]{3,2,1,0:T(8,128)} %refs_2_.1, f32[8,512,128]{2,1,0:T(8,128)} %refs_3_.3, s32[8,512]{1,0:T(8,128)} %refs_4_.3, ...), custom_call_target="tpu_custom_call" | custom-call | tf_op jit(solution)/shard_map/last/pallas_call | solution.py:367
  66.3 13.0 %all_to_all.5 = f32[32,8,128]{2,1,0:T(8,128)S(1)} all-to-all(f32[32,8,128]{2,1,0:T(8,128)} %get-tuple-element.51), channel_id=1, replica_groups=mesh['inst'=4,'space'=8] {'inst','space'}, dimensions={0} | all-to-all | bytes 262144 | tf_op jit(solution)/shard_map/all_to_all | solution.py:371
  (49 shorter events, 5.8 us)
Async XLA Ops:
  3.0 8.9 %collective-permute-start.2 = (f32[8,6,8,128]{3,2,1,0:T(8,128)}, f32[8,6,8,128]{3,2,1,0:T(8,128)S(1)}, u32[]{:S(2)}, u32[]{:S(2)}) collective-permute-start(f32[8,6,8,128]{3,2,1,0:T(8,128)} %get-tuple-element.34), channel_id=1, source_target_pairs={{0,8},{8,0},{16,24},{24,16},{1,9},{9,1},{17,25},{25,17},{2,10},{10... | collective-permute-start | bytes 589832 | tf_op jit(solution)/shard_map/ppermute | solution.py:300
  5.9 10.8 %collective-permute-start.3 = (f32[8,6,8,128]{3,2,1,0:T(8,128)}, f32[8,6,8,128]{3,2,1,0:T(8,128)S(1)}, u32[]{:S(2)}, u32[]{:S(2)}) collective-permute-start(f32[8,6,8,128]{3,2,1,0:T(8,128)} %get-tuple-element.35), channel_id=1, source_target_pairs={{0,16},{8,24},{16,0},{24,8},{1,17},{9,25},{17,1},{25,9},{2,18},{10... | collective-permute-start | bytes 589832 | tf_op jit(solution)/shard_map/ppermute | solution.py:300
  7.5 9.3 %collective-permute-start.4 = (f32[8,6,8,128]{3,2,1,0:T(8,128)}, f32[8,6,8,128]{3,2,1,0:T(8,128)S(1)}, u32[]{:S(2)}, u32[]{:S(2)}) collective-permute-start(f32[8,6,8,128]{3,2,1,0:T(8,128)} %get-tuple-element.36), channel_id=1, source_target_pairs={{0,24},{8,16},{16,8},{24,0},{1,25},{9,17},{17,9},{25,1},{2,26},{10... | collective-permute-start | bytes 589832 | tf_op jit(solution)/shard_map/ppermute | solution.py:300
  7.5 16.3 %collective-permute-start = (f32[8,6,8,128]{3,2,1,0:T(8,128)}, f32[8,6,8,128]{3,2,1,0:T(8,128)S(1)}, u32[]{:S(2)}, u32[]{:S(2)}) collective-permute-start(f32[8,6,8,128]{3,2,1,0:T(8,128)} %get-tuple-element.27), channel_id=1, source_target_pairs={{0,1},{1,2},{2,3},{3,4},{4,5},{5,6},{6,7},{7,0},{8,9},{9,10},{10,1... | collective-permute-start | bytes 589832 | tf_op jit(solution)/shard_map/ppermute | solution.py:306
  7.5 16.3 %collective-permute-start.1 = (f32[8,6,8,128]{3,2,1,0:T(8,128)}, f32[8,6,8,128]{3,2,1,0:T(8,128)S(1)}, u32[]{:S(2)}, u32[]{:S(2)}) collective-permute-start(f32[8,6,8,128]{3,2,1,0:T(8,128)} %get-tuple-element.28), channel_id=1, source_target_pairs={{1,0},{2,1},{3,2},{4,3},{5,4},{6,5},{7,6},{0,7},{9,8},{10,9},{11,1... | collective-permute-start | bytes 589832 | tf_op jit(solution)/shard_map/ppermute | solution.py:307
  11.9 4.8 %copy-start.9 = (f32[8,6,8,128]{3,2,1,0:T(8,128)}, f32[8,6,8,128]{3,2,1,0:T(8,128)S(1)}, u32[]{:S(2)}) copy-start(f32[8,6,8,128]{3,2,1,0:T(8,128)S(1)} %collective-permute-done.2.refs_2_) | copy-start | bytes 589828
  16.7 0.8 copy-start.11
  20.3 15.1 %collective-permute-start.5 = (f32[8,6,8,128]{3,2,1,0:T(8,128)}, f32[8,6,8,128]{3,2,1,0:T(8,128)S(1)}, u32[]{:S(2)}, u32[]{:S(2)}) collective-permute-start(f32[8,6,8,128]{3,2,1,0:T(8,128)} %get-tuple-element.38.refs_6_), channel_id=1, source_target_pairs={{0,8},{8,0},{16,24},{24,16},{1,9},{9,1},{17,25},{25,17},{2,10},{10... | collective-permute-start | bytes 589832 | tf_op jit(solution)/shard_map/ppermute | solution.py:300
  21.5 15.4 %collective-permute-start.6 = (f32[8,6,8,128]{3,2,1,0:T(8,128)}, f32[8,6,8,128]{3,2,1,0:T(8,128)S(1)}, u32[]{:S(2)}, u32[]{:S(2)}) collective-permute-start(f32[8,6,8,128]{3,2,1,0:T(8,128)} %get-tuple-element.39.refs_7_), channel_id=1, source_target_pairs={{0,16},{8,24},{16,0},{24,8},{1,17},{9,25},{17,1},{25,9},{2,18},{10... | collective-permute-start | bytes 589832 | tf_op jit(solution)/shard_map/ppermute | solution.py:300
  22.4 14.4 %collective-permute-start.7 = (f32[8,6,8,128]{3,2,1,0:T(8,128)}, f32[8,6,8,128]{3,2,1,0:T(8,128)S(1)}, u32[]{:S(2)}, u32[]{:S(2)}) collective-permute-start(f32[8,6,8,128]{3,2,1,0:T(8,128)} %get-tuple-element.40.refs_8_), channel_id=1, source_target_pairs={{0,24},{8,16},{16,8},{24,0},{1,25},{9,17},{17,9},{25,1},{2,26},{10... | collective-permute-start | bytes 589832 | tf_op jit(solution)/shard_map/ppermute | solution.py:300
  33.3 10.5 %collective-permute-start.10 = (f32[8,6,8,128]{3,2,1,0:T(8,128)}, f32[8,6,8,128]{3,2,1,0:T(8,128)S(1)}, u32[]{:S(2)}, u32[]{:S(2)}) collective-permute-start(f32[8,6,8,128]{3,2,1,0:T(8,128)} %get-tuple-element.30.refs_1_), channel_id=1, source_target_pairs={{0,8},{8,0},{16,24},{24,16},{1,9},{9,1},{17,25},{25,17},{2,10},{10... | collective-permute-start | bytes 589832 | tf_op jit(solution)/shard_map/ppermute | solution.py:300
  34.5 9.3 %collective-permute-start.11 = (f32[8,6,8,128]{3,2,1,0:T(8,128)}, f32[8,6,8,128]{3,2,1,0:T(8,128)S(1)}, u32[]{:S(2)}, u32[]{:S(2)}) collective-permute-start(f32[8,6,8,128]{3,2,1,0:T(8,128)} %get-tuple-element.31.refs_2_), channel_id=1, source_target_pairs={{0,16},{8,24},{16,0},{24,8},{1,17},{9,25},{17,1},{25,9},{2,18},{10... | collective-permute-start | bytes 589832 | tf_op jit(solution)/shard_map/ppermute | solution.py:300
  35.4 1.4 %copy-start.5 = (f32[8,6,8,128]{3,2,1,0:T(8,128)}, f32[8,6,8,128]{3,2,1,0:T(8,128)S(1)}, u32[]{:S(2)}) copy-start(f32[8,6,8,128]{3,2,1,0:T(8,128)S(1)} %collective-permute-done.5.refs_5_) | copy-start | bytes 589828
  35.4 8.4 %collective-permute-start.12 = (f32[8,6,8,128]{3,2,1,0:T(8,128)}, f32[8,6,8,128]{3,2,1,0:T(8,128)S(1)}, u32[]{:S(2)}, u32[]{:S(2)}) collective-permute-start(f32[8,6,8,128]{3,2,1,0:T(8,128)} %get-tuple-element.32.refs_3_), channel_id=1, source_target_pairs={{0,24},{8,16},{16,8},{24,0},{1,25},{9,17},{17,9},{25,1},{2,26},{10... | collective-permute-start | bytes 589832 | tf_op jit(solution)/shard_map/ppermute | solution.py:300
  36.8 0.8 copy-start.8
  40.2 11.6 %collective-permute-start.8 = (f32[8,6,8,128]{3,2,1,0:T(8,128)}, f32[8,6,8,128]{3,2,1,0:T(8,128)S(1)}, u32[]{:S(2)}, u32[]{:S(2)}) collective-permute-start(f32[8,6,8,128]{3,2,1,0:T(8,128)} %get-tuple-element.42), channel_id=1, source_target_pairs={{0,1},{1,2},{2,3},{3,4},{4,5},{5,6},{6,7},{7,0},{8,9},{9,10},{10,1... | collective-permute-start | bytes 589832 | tf_op jit(solution)/shard_map/ppermute | solution.py:306
  40.3 11.6 %collective-permute-start.9 = (f32[8,6,8,128]{3,2,1,0:T(8,128)}, f32[8,6,8,128]{3,2,1,0:T(8,128)S(1)}, u32[]{:S(2)}, u32[]{:S(2)}) collective-permute-start(f32[8,6,8,128]{3,2,1,0:T(8,128)} %get-tuple-element.43), channel_id=1, source_target_pairs={{1,0},{2,1},{3,2},{4,3},{5,4},{6,5},{7,6},{0,7},{9,8},{10,9},{11,1... | collective-permute-start | bytes 589832 | tf_op jit(solution)/shard_map/ppermute | solution.py:307
  43.8 0.8 copy-start.4
  48.3 12.5 %collective-permute-start.13 = (f32[8,6,8,128]{3,2,1,0:T(8,128)}, f32[8,6,8,128]{3,2,1,0:T(8,128)S(1)}, u32[]{:S(2)}, u32[]{:S(2)}) collective-permute-start(f32[8,6,8,128]{3,2,1,0:T(8,128)} %get-tuple-element.47), channel_id=1, source_target_pairs={{0,8},{8,0},{16,24},{24,16},{1,9},{9,1},{17,25},{25,17},{2,10},{10... | collective-permute-start | bytes 589832 | tf_op jit(solution)/shard_map/ppermute | solution.py:300
  49.5 11.3 %collective-permute-start.14 = (f32[8,6,8,128]{3,2,1,0:T(8,128)}, f32[8,6,8,128]{3,2,1,0:T(8,128)S(1)}, u32[]{:S(2)}, u32[]{:S(2)}) collective-permute-start(f32[8,6,8,128]{3,2,1,0:T(8,128)} %get-tuple-element.48), channel_id=1, source_target_pairs={{0,16},{8,24},{16,0},{24,8},{1,17},{9,25},{17,1},{25,9},{2,18},{10... | collective-permute-start | bytes 589832 | tf_op jit(solution)/shard_map/ppermute | solution.py:300
  50.5 10.3 %collective-permute-start.15 = (f32[8,6,8,128]{3,2,1,0:T(8,128)}, f32[8,6,8,128]{3,2,1,0:T(8,128)S(1)}, u32[]{:S(2)}, u32[]{:S(2)}) collective-permute-start(f32[8,6,8,128]{3,2,1,0:T(8,128)} %get-tuple-element.49), channel_id=1, source_target_pairs={{0,24},{8,16},{16,8},{24,0},{1,25},{9,17},{17,9},{25,1},{2,26},{10... | collective-permute-start | bytes 589832 | tf_op jit(solution)/shard_map/ppermute | solution.py:300
  51.8 0.8 copy-start.14
  60.8 0.8 copy-start.1
  60.8 0.8 %copy-start.2 = (f32[8,6,8,128]{3,2,1,0:T(8,128)}, f32[8,6,8,128]{3,2,1,0:T(8,128)S(1)}, u32[]{:S(2)}) copy-start(f32[8,6,8,128]{3,2,1,0:T(8,128)S(1)} %collective-permute-done.15.refs_8_) | copy-start | bytes 589828
  (8 other events, 5.4 us)

commit v2 on v1

v2 whole, which is shorter than its diff:
```python
import math

import jax
import jax.numpy as jnp
import numpy as np
from jax import lax
from jax.experimental import pallas as pl
from jax.experimental.pallas import tpu as pltpu
from jax.sharding import PartitionSpec as P

NT = 32
PATCH_DEV = 8
REACH = 16
LANES = 128
SCALE = 0.1
F32 = jnp.float32
SCRATCH_LIMIT = 4 << 20


def weight_matrix(count):
    weights = np.zeros((count, count))
    for s in range(count):
        for t in range(count):
            if s != t:
                angle = math.pi * (s - t) / count
                weights[s, t] = 0.5 * (-1.0) ** (s - t) * math.cos(angle) / math.sin(angle)
    return weights


def circulant_apply(values):
    count = len(values)
    row = weight_matrix(count)[:, 0]
    if count == 2:
        return None
    half = count // 2
    total = [values[s] + values[s + half] for s in range(half)]
    diff = [values[s] - values[s + half] for s in range(half)]
    even = circulant_apply(total)
    q = [(row[d] - row[d + half]) / 2 for d in range(half)]
    quarter = half // 2

    def at(position):
        position %= count
        return (diff[position], 1.0) if position < half else (diff[position - half], -1.0)

    out = [None] * count
    for t in range(half):
        acc = None
        for d in range(1, quarter):
            plus, sign_plus = at(t + d)
            minus, sign_minus = at(t - d)
            pair = plus - minus if sign_plus == sign_minus else plus + minus
            term = float(q[d] * sign_plus) * pair
            acc = term if acc is None else acc + term
        last, sign = at(t + quarter)
        term = float(q[quarter] * sign) * last
        acc = term if acc is None else acc + term
        if even is None:
            out[t], out[t + half] = acc, -acc
        else:
            out[t], out[t + half] = even[t] + acc, even[t] - acc
    return out


def chunk_place(chunk, n_inst, nv, ny):
    split = n_inst // (ny // LANES)
    return (chunk // split, (chunk % split) * (nv // split)) if split > 1 else (chunk, 0)


def lane_tile(index):
    return pl.ds(pl.multiple_of(index * LANES, LANES), LANES)


def pack_rows(row_block, first_row, ny):
    tiles = ny // LANES
    sub = lax.broadcasted_iota(jnp.int32, (8, LANES), 0)
    packed = None
    for y in range(tiles):
        tile = row_block[:, y * LANES : (y + 1) * LANES]
        shift = (2 * y - first_row) % 8
        moved = pltpu.roll(tile, shift, 0) if shift else tile
        packed = moved if packed is None else jnp.where(sub >= 2 * y, moved, packed)
    return packed


def pack_kernel(n_inst, a_hbm, a_ref, *refs):
    chunks, (first_ref, last_ref, arrived) = refs[:n_inst], refs[n_inst:]
    steps, nv, _, ny = a_ref.shape
    me = lax.axis_index("inst")

    def copy(t):
        return pltpu.make_async_copy(a_hbm.at[t], a_ref.at[t], arrived.at[t])

    for t in range(steps):
        copy(t).start()

    def at_step(t, _):
        copy(t).wait()
        for r in range(n_inst):
            y, k0 = chunk_place(me ^ r, n_inst, nv, ny)
            for k in range(chunks[0].shape[1]):
                chunks[r][t, k] = a_ref[t, k0 + k, :, lane_tile(y)]
        pack_edges(t, a_ref, first_ref, last_ref)
        return 0

    lax.fori_loop(0, steps, at_step, 0)


def pack_edges(t, a_ref, first_ref, last_ref):
    _, nv, _, ny = a_ref.shape
    for k in range(nv):
        rows = a_ref[t, k]
        first_ref[t, k] = pack_rows(rows, 0, ny)
        last_ref[t, k] = pack_rows(rows, 6, ny)


def chord_terms(t, a_ref, src_ref, fy_ref, acc_ref, chord):
    _, nv, rows, ny = a_ref.shape
    lane = lax.broadcasted_iota(jnp.int32, (rows, ny), 1)
    for k in range(nv):
        a = a_ref[t, k]
        above = jnp.where(lane == ny - 1, 0.0, pltpu.roll(a, ny - 1, 1))
        below = jnp.where(lane == 0, 0.0, pltpu.roll(a, 1, 1))
        chord[k] = above - below
        acc_ref[t, k] = src_ref[t, k] + (above + below)
    for y in range(ny // LANES):
        lanes = slice(y * LANES, (y + 1) * LANES)
        tiles = [chord[j, :, lanes] for j in range(nv)]
        for k in range(nv):
            total = fy_ref[t, 0, k, :, lanes] * tiles[0]
            for j in range(1, nv):
                total = total + fy_ref[t, j, k, :, lanes] * tiles[j]
            acc_ref[t, k, :, lanes] = acc_ref[t, k, :, lanes] - total


def first_chord_kernel(
    a_ref, src_hbm, d_hbm, fx_hbm, fy_hbm,
    acc_ref, src_ref, inverse, fx_ref, fy_ref, chord, d_ref, arrived, d_arrived,
):
    steps = a_ref.shape[0]

    pairs = ((src_hbm, src_ref), (fy_hbm, fy_ref), (fx_hbm, fx_ref))

    def copy(i, t):
        there, here = pairs[i]
        return pltpu.make_async_copy(there.at[t], here.at[t], arrived.at[i, t])

    d_copy = pltpu.make_async_copy(d_hbm, d_ref, d_arrived)
    for t in range(steps):
        copy(0, t).start()
        copy(1, t).start()
    d_copy.start()
    for t in range(steps):
        copy(2, t).start()

    def at_step(t, _):
        copy(0, t).wait()
        copy(1, t).wait()
        chord_terms(t, a_ref, src_ref, fy_ref, acc_ref, chord)
        return 0

    lax.fori_loop(0, steps, at_step, 0)
    d_copy.wait()
    inverse[...] = 1.0 / d_ref[...]
    for t in range(steps):
        copy(2, t).wait()


def second_chord_kernel(a_ref, src_ref, fy_ref, acc_ref, chord):
    def at_step(t, _):
        chord_terms(t, a_ref, src_ref, fy_ref, acc_ref, chord)
        return 0

    lax.fori_loop(0, a_ref.shape[0], at_step, 0)


def pitch_terms(t, a_ref, prev_ref, next_ref, pitch, near):
    nv, rows, ny = pitch.shape
    tiles = ny // LANES
    sub = lax.broadcasted_iota(jnp.int32, (rows, LANES), 0)
    for k in range(nv):
        before, after = prev_ref[t, k], next_ref[t, k]
        for y in range(tiles):
            lanes = slice(y * LANES, (y + 1) * LANES)
            a = a_ref[t, k, :, lanes]
            low = pltpu.roll(before, (-2 * y) % 8, 0) if y else before
            high = pltpu.roll(after, (6 - 2 * y) % 8, 0) if (6 - 2 * y) % 8 else after
            edge = jnp.where(sub < 4, low, high)
            plus_two = jnp.where(sub >= 6, edge, pltpu.roll(a, 6, 0))
            plus_one = jnp.where(sub == 7, pltpu.roll(edge, 1, 0), pltpu.roll(a, 7, 0))
            minus_two = jnp.where(sub < 2, edge, pltpu.roll(a, 2, 0))
            minus_one = jnp.where(sub == 0, pltpu.roll(edge, 7, 0), pltpu.roll(a, 1, 0))
            pitch[k, :, lanes] = (
                2.0 / 3.0 * (plus_one - minus_one) - 1.0 / 12.0 * (plus_two - minus_two)
            )
            near[k, :, lanes] = plus_one + minus_one


def swept_tile(t, k, lanes, acc_ref, fx_ref, pitch_tiles, near, inverse):
    total = acc_ref[t, k, :, lanes] + near[k, :, lanes]
    for j in range(len(pitch_tiles)):
        total = total - fx_ref[t, j, k, :, lanes] * pitch_tiles[j]
    return total * inverse[k, :, lanes]


def first_pitch_kernel(n_inst, a_ref, prev_ref, next_ref, acc_ref, fx_ref, inverse, *refs):
    out_refs, (pitch, near) = refs[:n_inst], refs[n_inst:]
    nv, _, ny = pitch.shape
    part = out_refs[0].shape[1]
    me = lax.axis_index("inst")

    def at_step(t, _):
        pitch_terms(t, a_ref, prev_ref, next_ref, pitch, near)
        for r in range(n_inst):
            y, k0 = chunk_place(me ^ r, n_inst, nv, ny)
            lanes = lane_tile(y)
            pitch_tiles = [pitch[j, :, lanes] for j in range(nv)]
            for k in range(part):
                out_refs[r][t, k] = swept_tile(
                    t, k0 + k, lanes, acc_ref, fx_ref, pitch_tiles, near, inverse
                )
        return 0

    lax.fori_loop(0, a_ref.shape[0], at_step, 0)


def spectral_kernel(n_inst, second, inverse, *refs):
    in_refs = refs[:n_inst]
    shift_refs = refs[n_inst : 2 * n_inst] if second else ()
    out_refs = refs[(2 if second else 1) * n_inst : (3 if second else 2) * n_inst]
    (work,) = refs[(3 if second else 2) * n_inst :]
    per, part = in_refs[0].shape[:2]
    nv, _, ny = inverse.shape
    me = lax.axis_index("inst")
    y, k0 = chunk_place(me, n_inst, nv, ny)

    def at_tile(c, _):
        for r in range(n_inst):
            base = (me ^ r) * per
            for t in range(per):
                value = in_refs[r][t, c]
                if second:
                    value = value - shift_refs[r][t, c]
                work[base + t] = value
        out = circulant_apply([work[s] for s in range(NT)])
        factor = SCALE * inverse[k0 + c, :, lane_tile(y)]
        for s in range(NT):
            work[s] = out[s] * factor
        for r in range(n_inst):
            base = (me ^ r) * per
            for t in range(per):
                out_refs[r][t, c] = work[base + t]
        return 0

    lax.fori_loop(0, part, at_tile, 0)


def join_kernel(n_inst, *refs):
    b_refs, z_refs = refs[:n_inst], refs[n_inst : 2 * n_inst]
    a_ref, first_ref, last_ref = refs[2 * n_inst :]
    steps, nv, _, ny = a_ref.shape
    me = lax.axis_index("inst")

    def at_step(t, _):
        for r in range(n_inst):
            y, k0 = chunk_place(me ^ r, n_inst, nv, ny)
            for k in range(b_refs[0].shape[1]):
                a_ref[t, k0 + k, :, lane_tile(y)] = b_refs[r][t, k] - z_refs[r][t, k]
        pack_edges(t, a_ref, first_ref, last_ref)
        return 0

    lax.fori_loop(0, steps, at_step, 0)


def second_pitch_kernel(
    a_ref, prev_ref, next_ref, acc_ref, fx_ref, inverse, shape_ref, out_ref, weight_ref, pitch, near
):
    nv, _, ny = pitch.shape
    weight_ref[...] = jnp.zeros_like(weight_ref)

    def at_step(t, _):
        pitch_terms(t, a_ref, prev_ref, next_ref, pitch, near)
        for y in range(ny // LANES):
            lanes = slice(y * LANES, (y + 1) * LANES)
            pitch_tiles = [pitch[j, :, lanes] for j in range(nv)]
            weight = weight_ref[:, lanes]
            for k in range(nv):
                value = swept_tile(t, k, lanes, acc_ref, fx_ref, pitch_tiles, near, inverse)
                out_ref[t, k, :, lanes] = value
                weight = weight + value * shape_ref[t, k, :, lanes]
            weight_ref[:, lanes] = weight
        return 0

    lax.fori_loop(0, a_ref.shape[0], at_step, 0)


def last_kernel(n_inst, x_ref, weight_ref, shape_ref, mode_ref, patch_ref, *refs):
    z_refs, (a_ref, send_ref, weight) = refs[:n_inst], refs[n_inst:]
    steps, nv, rows, ny = x_ref.shape
    part = z_refs[0].shape[1]
    me, space = lax.axis_index("inst"), lax.axis_index("space")
    owners = send_ref.shape[0]
    per_space = PATCH_DEV * n_inst
    window = per_space + 2 * REACH
    weight[...] = weight_ref[...]

    def at_step(t, _):
        for r in range(n_inst):
            y, k0 = chunk_place(me ^ r, n_inst, nv, ny)
            total = jnp.zeros((rows, LANES), F32)
            for k in range(part):
                z = z_refs[r][t, k]
                a_ref[t, k0 + k, :, lane_tile(y)] = (
                    x_ref[t, k0 + k, :, lane_tile(y)] - z
                )
                total = total + z * shape_ref[t, k0 + k, :, lane_tile(y)]
            weight[:, lane_tile(y)] = weight[:, lane_tile(y)] - total
        return 0

    lax.fori_loop(0, steps, at_step, 0)
    first = per_space * space - REACH
    ids = lax.broadcasted_iota(jnp.int32, (window, ny), 0) + first
    acc = jnp.zeros((window, LANES), F32)
    for x in range(rows):
        hit = jnp.where(ids == patch_ref[x : x + 1, :], weight[x : x + 1, :], 0.0)
        acc = acc + jnp.dot(
            hit, mode_ref[x], precision=lax.Precision.HIGHEST, preferred_element_type=F32
        )
    send_ref[...] = jnp.zeros_like(send_ref)
    first_owner = n_inst * space - REACH // PATCH_DEV
    for j in range(window // PATCH_DEV):
        owner = first_owner + j

        @pl.when((owner >= 0) & (owner < owners))
        def _():
            send_ref[owner] = acc[j * PATCH_DEV : (j + 1) * PATCH_DEV]


def call(kernel, outs, scratch=(), n_hbm=None, name=None):
    n_hbm = n_hbm or ()
    scratch_shapes = [pltpu.VMEM(x, F32) if isinstance(x, tuple) else x for x in scratch]

    def run(*args):
        return pl.pallas_call(
            kernel,
            out_shape=[pltpu.VMEM(shape, F32) for shape in outs],
            in_specs=[
                pl.BlockSpec(memory_space=pltpu.HBM if i in n_hbm else pltpu.VMEM)
                for i in range(len(args))
            ],
            scratch_shapes=scratch_shapes,
            compiler_params=pltpu.CompilerParams(vmem_limit_bytes=SCRATCH_LIMIT),
            name=name,
        )(
            *(
                pltpu.with_memory_space_constraint(x, pltpu.HBM if i in n_hbm else pltpu.VMEM)
                for i, x in enumerate(args)
            )
        )

    return run


def make_body(n_inst, n_space):
    def exchange(chunks):
        return [chunks[0]] + [
            lax.ppermute(chunks[r], "inst", [(i, i ^ r) for i in range(n_inst)])
            for r in range(1, n_inst)
        ]

    def edges(first, last):
        ring = [(i, (i + 1) % n_space) for i in range(n_space)]
        before = lax.ppermute(last, "space", ring)
        after = lax.ppermute(first, "space", [(j, i) for i, j in ring])
        return before, after

    def body(start, source, diagonal, flux_x, flux_y, shape_derivative, mode_basis, patch_of_cell):
        steps, nv, rows, ny = start.shape
        part = nv * (ny // LANES) // n_inst
        chunk = (steps, part, 8, LANES)
        edge = (steps, nv, 8, LANES)
        tile = (nv, rows, ny)

        def bound(kernel, *args):
            def run(*refs):
                kernel(*args, *refs)

            return run

        a0, *chunks, first, last = call(
            bound(pack_kernel, n_inst), [start.shape] + [chunk] * n_inst + [edge] * 2,
            scratch=[pltpu.SemaphoreType.DMA((steps,))], n_hbm=(0,), name="pack",
        )(start)
        before, after = edges(first, last)
        start_cells = exchange(chunks)
        acc, src, inverse, fx, fy = call(
            first_chord_kernel,
            [start.shape, source.shape, tile, flux_x.shape, flux_y.shape],
            scratch=[
                tile, tile, pltpu.SemaphoreType.DMA((3, steps)), pltpu.SemaphoreType.DMA(())
            ],
            n_hbm=(1, 2, 3, 4), name="chord1",
        )(a0, source, diagonal, flux_x, flux_y)
        b = call(
            bound(first_pitch_kernel, n_inst), [chunk] * n_inst, scratch=[tile, tile], name="pitch1"
        )(a0, before, after, acc, fx, inverse)
        b_cells = exchange(b)
        z0_cells = call(
            bound(spectral_kernel, n_inst, False), [chunk] * n_inst, scratch=[(NT, 8, LANES)],
            name="spectral1",
        )(inverse, *start_cells)
        z0 = exchange(z0_cells)
        z1_cells = call(
            bound(spectral_kernel, n_inst, True), [chunk] * n_inst, scratch=[(NT, 8, LANES)],
            name="spectral2",
        )(inverse, *b_cells, *z0_cells)
        z1 = exchange(z1_cells)
        a1, first, last = call(
            bound(join_kernel, n_inst), [start.shape, edge, edge], name="join"
        )(*b, *z0)
        before, after = edges(first, last)
        (acc,) = call(second_chord_kernel, [start.shape], scratch=[tile], name="chord2")(
            a1, src, fy
        )
        x, weight = call(
            second_pitch_kernel, [start.shape, (rows, ny)], scratch=[tile, tile], name="pitch2"
        )(a1, before, after, acc, fx, inverse, shape_derivative)
        owners = n_inst * n_space
        adjoint, sends = call(
            bound(last_kernel, n_inst), [start.shape, (owners, PATCH_DEV, LANES)],
            scratch=[(rows, ny)], name="last",
        )(x, weight, shape_derivative, mode_basis, patch_of_cell, *z1)
        parts = lax.all_to_all(sends, ("inst", "space"), 0, 0, tiled=True)
        return adjoint, jnp.sum(parts, axis=0)

    return body


def solution(mesh):
    placed = (
        P("inst", None, "space", None),
        P("inst", None, "space", None),
        P(None, "space", None),
        P("inst", None, None, "space", None),
        P("inst", None, None, "space", None),
        P("inst", None, "space", None),
        P("space", None, None),
        P("space", None),
    )
    return jax.shard_map(
        make_body(mesh.shape["inst"], mesh.shape["space"]),
        mesh=mesh,
        in_specs=placed,
        out_specs=(P("inst", None, "space", None), P(("inst", "space"), None)),
        check_vma=False,
    )
```

time: 80.6 us -> 61.8 us (0.77)
  Pallas kernels: 31.9 us -> 13.1 us
  blocking collectives: 13 us -> 0 us
  waiting for transfers between devices: 5.75 us -> 18.1 us
  starting transfers between devices: 22.1 us -> 28.1 us
  local copies, waits for them, and re-layouts: 5.87 us -> 0.9 us
    pallas_call x7 -> x9, Pallas kernels: 31.9 us -> 13.1 us  [run(): pl.pallas_call(kernel, out_shape=[pltpu.VMEM(shape, F32) for shape in out...]
    all_to_all x1 -> x0, blocking collectives: 13 us -> none  [body(): parts = lax.all_to_all(sends, ('inst', 'space'), 0, 0, tiled=True)]
    all_to_all x0 -> x1, waiting for transfers between devices: none -> 7.28 us  [body(): parts = lax.all_to_all(sends, ('inst', 'space'), 0, 0, tiled=True)]
    ppermute x12, waiting for transfers between devices: 5.74 us -> 10.8 us  [exchange(): lax.ppermute(chunks[r], 'inst', [(i, i ^ r) for i in range(n_inst)])]
    unnamed x32 -> x7, local copies, waits for them, and re-layouts: 5.87 us -> 0.9 us
    all_to_all x0 -> x1, starting transfers between devices: none -> 4.9 us  [body(): parts = lax.all_to_all(sends, ('inst', 'space'), 0, 0, tiled=True)]
    ppermute x12, starting transfers between devices: 15 us -> 16.1 us  [exchange(): lax.ppermute(chunks[r], 'inst', [(i, i ^ r) for i in range(n_inst)])]
  transfers between devices with their start and end apart: 16 -> 17, of which waited for: 2 -> 7; matrix products, arithmetic and copies ran while one was open for 0% -> 1% of each run, Pallas kernels for 31% -> 16%
where the time goes in v2:
time: 61.8 us; the launch traced here: 61.6 us
  starting transfers between devices  28.1 us (45%)
  waiting for transfers between devices  18.1 us (29%)
  Pallas kernels  13.1 us (21%)
  local copies, waits for them, and re-layouts  0.9 us (1%)
  between operations  0.78 us (1%)
  other arithmetic  0.63 us (1%)
    ppermute x12, starting transfers between devices, exchange(): lax.ppermute(chunks[r], 'inst', [(i, i ^ r) for i in range(n_inst)])  16.1 us
    pallas_call x9, Pallas kernels, run(): pl.pallas_call(kernel, out_shape=[pltpu.VMEM(shape, F32) for shape in out...  13.1 us
    ppermute x12, waiting for transfers between devices, exchange(): lax.ppermute(chunks[r], 'inst', [(i, i ^ r) for i in range(n_inst)])  10.8 us
    all_to_all x1, waiting for transfers between devices, body(): parts = lax.all_to_all(sends, ('inst', 'space'), 0, 0, tiled=True)  7.28 us
    ppermute x2, starting transfers between devices, edges(): after = lax.ppermute(first, 'space', [(j, i) for i, j in ring])  7.07 us
    all_to_all x1, starting transfers between devices, body(): parts = lax.all_to_all(sends, ('inst', 'space'), 0, 0, tiled=True)  4.9 us
  transfers between devices with their start and end apart: 17, of which 7 were waited for; matrix products, arithmetic and copies ran while one was open for 1% of the time, Pallas kernels for 16%

profile of v2, /device:TPU:0, one launch (start us, length us, event | category | flops | bytes accessed | tf_op | source)
XLA Modules:
  0.0 61.6 jit_solution(6402181981819665423)
XLA Ops:
  0.6 1.3 %pack.1 = (f32[8,6,8,512]{3,2,1,0:T(8,128)S(1)}, f32[8,6,8,128]{3,2,1,0:T(8,128)S(1)}, f32[8,6,8,128]{3,2,1,0:T(8,128)S(1)}, f32[8,6,8,128]{3,2,1,0:T(8,128)S(1)...) custom-call(f32[8,6,8,512]{3,2,1,0:T(8,128)} %refs_0_.1), custom_call_target="tpu_custom_call" | custom-call | tf_op jit(solution)/shard_map/pack/pallas_call | solution.py:344
  1.9 3.0 %collective-permute-start.2 = (f32[8,6,8,128]{3,2,1,0:T(8,128)S(1)}, f32[8,6,8,128]{3,2,1,0:T(8,128)S(1)}, u32[]{:S(2)}, u32[]{:S(2)}) collective-permute-start(f32[8,6,8,128]{3,2,1,0:T(8,128)S(1)} %get-tuple-element.44), channel_id=1, source_target_pairs={{0,8},{8,0},{16,24},{24,16},{1,9},{9,1},{17,25},{25,17},{2,10},{10... | collective-permute-start | bytes 589832 | tf_op jit(solution)/shard_map/ppermute | solution.py:367
  5.0 1.5 %collective-permute-start.3 = (f32[8,6,8,128]{3,2,1,0:T(8,128)S(1)}, f32[8,6,8,128]{3,2,1,0:T(8,128)S(1)}, u32[]{:S(2)}, u32[]{:S(2)}) collective-permute-start(f32[8,6,8,128]{3,2,1,0:T(8,128)S(1)} %get-tuple-element.45), channel_id=1, source_target_pairs={{0,16},{8,24},{16,0},{24,8},{1,17},{9,25},{17,1},{25,9},{2,18},{10... | collective-permute-start | bytes 589832 | tf_op jit(solution)/shard_map/ppermute | solution.py:367
  6.5 3.5 %collective-permute-start.1 = (f32[8,6,8,128]{3,2,1,0:T(8,128)S(1)}, f32[8,6,8,128]{3,2,1,0:T(8,128)S(1)}, u32[]{:S(2)}, u32[]{:S(2)}) collective-permute-start(f32[8,6,8,128]{3,2,1,0:T(8,128)S(1)} %get-tuple-element.35), channel_id=1, source_target_pairs={{1,0},{2,1},{3,2},{4,3},{5,4},{6,5},{7,6},{0,7},{9,8},{10,9},{11,1... | collective-permute-start | bytes 589832 | tf_op jit(solution)/shard_map/ppermute | solution.py:374
  10.1 4.3 %chord1.1 = (f32[8,6,8,512]{3,2,1,0:T(8,128)S(1)}, f32[8,6,8,512]{3,2,1,0:T(8,128)S(1)}, f32[6,8,512]{2,1,0:T(8,128)S(1)}, f32[8,6,6,8,512]{4,3,2,1,0:T(8,128)S(1)}, f32[8,6,6,8,512]{4,3,2,1,0:T(8,128)S(1)}) custom-call(f32[8,6,8,512]{3,2,1,0:T(8,128)S(1)} %get-tuple-element.33.a_ref.refs_0_, f32[8,6,8,512]{3,2,1,0:T(8,128)} %src_hbm.1, f32[6,8,512]{2,1,0:T(8,128)} %d_hbm.1, ...), custom_call_target="tpu_custom_call" | custom-call | tf_op jit(solution)/shard_map/chord1/pallas_call | solution.py:344
  14.4 1.2 %collective-permute-done.3.refs_3_ = f32[8,6,8,128]{3,2,1,0:T(8,128)S(1)} collective-permute-done((f32[8,6,8,128]{3,2,1,0:T(8,128)S(1)}, f32[8,6,8,128]{3,2,1,0:T(8,128)S(1)}, u32[]{:S(2)}, u32[]{:S(2)}) %collective-permute-start.3) | collective-permute-done | bytes 196640 | tf_op jit(solution)/shard_map/ppermute | solution.py:367
  16.2 1.3 %collective-permute-start.5 = (f32[8,6,8,128]{3,2,1,0:T(8,128)S(1)}, f32[8,6,8,128]{3,2,1,0:T(8,128)S(1)}, u32[]{:S(2)}, u32[]{:S(2)}) collective-permute-start(f32[8,6,8,128]{3,2,1,0:T(8,128)S(1)} %get-tuple-element.48.refs_6_), channel_id=1, source_target_pairs={{0,8},{8,0},{16,24},{24,16},{1,9},{9,1},{17,25},{25,17},{2,10},{10... | collective-permute-start | bytes 589832 | tf_op jit(solution)/shard_map/ppermute | solution.py:367
  17.5 1.1 %collective-permute-start.6 = (f32[8,6,8,128]{3,2,1,0:T(8,128)S(1)}, f32[8,6,8,128]{3,2,1,0:T(8,128)S(1)}, u32[]{:S(2)}, u32[]{:S(2)}) collective-permute-start(f32[8,6,8,128]{3,2,1,0:T(8,128)S(1)} %get-tuple-element.49.refs_7_), channel_id=1, source_target_pairs={{0,16},{8,24},{16,0},{24,8},{1,17},{9,25},{17,1},{25,9},{2,18},{10... | collective-permute-start | bytes 589832 | tf_op jit(solution)/shard_map/ppermute | solution.py:367
  18.6 1.1 %collective-permute-start.7 = (f32[8,6,8,128]{3,2,1,0:T(8,128)S(1)}, f32[8,6,8,128]{3,2,1,0:T(8,128)S(1)}, u32[]{:S(2)}, u32[]{:S(2)}) collective-permute-start(f32[8,6,8,128]{3,2,1,0:T(8,128)S(1)} %get-tuple-element.50.refs_8_), channel_id=1, source_target_pairs={{0,24},{8,16},{16,8},{24,0},{1,25},{9,17},{17,9},{25,1},{2,26},{10... | collective-permute-start | bytes 589832 | tf_op jit(solution)/shard_map/ppermute | solution.py:367
  19.8 1.4 %pitch1.1 = (f32[8,6,8,128]{3,2,1,0:T(8,128)S(1)}, f32[8,6,8,128]{3,2,1,0:T(8,128)S(1)}, f32[8,6,8,128]{3,2,1,0:T(8,128)S(1)}, f32[8,6,8,128]{3,2,1,0:T(8,128)S(1)}) custom-call(f32[8,6,8,512]{3,2,1,0:T(8,128)S(1)} %get-tuple-element.33.a_ref.refs_0_, f32[8,6,8,128]{3,2,1,0:T(8,128)S(1)} %collective-permute-done.refs_1_, ...), custom_call_target="tpu_custom_call" | custom-call | tf_op jit(solution)/shard_map/pitch1/pallas_call | solution.py:344
  21.2 1.3 %collective-permute-start.10 = (f32[8,6,8,128]{3,2,1,0:T(8,128)S(1)}, f32[8,6,8,128]{3,2,1,0:T(8,128)S(1)}, u32[]{:S(2)}, u32[]{:S(2)}) collective-permute-start(f32[8,6,8,128]{3,2,1,0:T(8,128)S(1)} %get-tuple-element.40.refs_1_), channel_id=1, source_target_pairs={{0,8},{8,0},{16,24},{24,16},{1,9},{9,1},{17,25},{25,17},{2,10},{10... | collective-permute-start | bytes 589832 | tf_op jit(solution)/shard_map/ppermute | solution.py:367
  22.5 1.1 %collective-permute-start.11 = (f32[8,6,8,128]{3,2,1,0:T(8,128)S(1)}, f32[8,6,8,128]{3,2,1,0:T(8,128)S(1)}, u32[]{:S(2)}, u32[]{:S(2)}) collective-permute-start(f32[8,6,8,128]{3,2,1,0:T(8,128)S(1)} %get-tuple-element.41.refs_2_), channel_id=1, source_target_pairs={{0,16},{8,24},{16,0},{24,8},{1,17},{9,25},{17,1},{25,9},{2,18},{10... | collective-permute-start | bytes 589832 | tf_op jit(solution)/shard_map/ppermute | solution.py:367
  23.9 2.0 %collective-permute-start.12 = (f32[8,6,8,128]{3,2,1,0:T(8,128)S(1)}, f32[8,6,8,128]{3,2,1,0:T(8,128)S(1)}, u32[]{:S(2)}, u32[]{:S(2)}) collective-permute-start(f32[8,6,8,128]{3,2,1,0:T(8,128)S(1)} %get-tuple-element.42.refs_3_), channel_id=1, source_target_pairs={{0,24},{8,16},{16,8},{24,0},{1,25},{9,17},{17,9},{25,1},{2,26},{10... | collective-permute-start | bytes 589832 | tf_op jit(solution)/shard_map/ppermute | solution.py:367
  25.8 3.6 %collective-permute-done.6.refs_6_ = f32[8,6,8,128]{3,2,1,0:T(8,128)S(1)} collective-permute-done((f32[8,6,8,128]{3,2,1,0:T(8,128)S(1)}, f32[8,6,8,128]{3,2,1,0:T(8,128)S(1)}, u32[]{:S(2)}, u32[]{:S(2)}) %collective-permute-start.6) | collective-permute-done | bytes 196640 | tf_op jit(solution)/shard_map/ppermute | solution.py:367
  29.7 3.5 %collective-permute-start.9 = (f32[8,6,8,128]{3,2,1,0:T(8,128)S(1)}, f32[8,6,8,128]{3,2,1,0:T(8,128)S(1)}, u32[]{:S(2)}, u32[]{:S(2)}) collective-permute-start(f32[8,6,8,128]{3,2,1,0:T(8,128)S(1)} %get-tuple-element.53), channel_id=1, source_target_pairs={{1,0},{2,1},{3,2},{4,3},{5,4},{6,5},{7,6},{0,7},{9,8},{10,9},{11,1... | collective-permute-start | bytes 589832 | tf_op jit(solution)/shard_map/ppermute | solution.py:374
  33.3 2.4 %collective-permute-done.11.refs_3_ = f32[8,6,8,128]{3,2,1,0:T(8,128)S(1)} collective-permute-done((f32[8,6,8,128]{3,2,1,0:T(8,128)S(1)}, f32[8,6,8,128]{3,2,1,0:T(8,128)S(1)}, u32[]{:S(2)}, u32[]{:S(2)}) %collective-permute-start.11) | collective-permute-done | bytes 196640 | tf_op jit(solution)/shard_map/ppermute | solution.py:367
  37.0 1.6 %collective-permute-start.14 = (f32[8,6,8,128]{3,2,1,0:T(8,128)S(1)}, f32[8,6,8,128]{3,2,1,0:T(8,128)S(1)}, u32[]{:S(2)}, u32[]{:S(2)}) collective-permute-start(f32[8,6,8,128]{3,2,1,0:T(8,128)S(1)} %get-tuple-element.60), channel_id=1, source_target_pairs={{0,16},{8,24},{16,0},{24,8},{1,17},{9,25},{17,1},{25,9},{2,18},{10... | collective-permute-start | bytes 589832 | tf_op jit(solution)/shard_map/ppermute | solution.py:367
  38.6 1.3 %collective-permute-start.15 = (f32[8,6,8,128]{3,2,1,0:T(8,128)S(1)}, f32[8,6,8,128]{3,2,1,0:T(8,128)S(1)}, u32[]{:S(2)}, u32[]{:S(2)}) collective-permute-start(f32[8,6,8,128]{3,2,1,0:T(8,128)S(1)} %get-tuple-element.61), channel_id=1, source_target_pairs={{0,24},{8,16},{16,8},{24,0},{1,25},{9,17},{17,9},{25,1},{2,26},{10... | collective-permute-start | bytes 589832 | tf_op jit(solution)/shard_map/ppermute | solution.py:367
  39.9 1.2 %chord2.1.acc_ref = f32[8,6,8,512]{3,2,1,0:T(8,128)S(1)} custom-call(f32[8,6,8,512]{3,2,1,0:T(8,128)S(1)} %get-tuple-element.51.a_ref, f32[8,6,8,512]{3,2,1,0:T(8,128)S(1)} %get-tuple-element.54.src_ref, f32[8,6,6,8,512]{4,3,2,1,0:T(8,128)S(1)} %get-tuple-element.55.fy_ref), custom_call_target="tpu_custom_call" | custom-call | tf_op jit(solution)/shard_map/chord2/pallas_call | solution.py:344
  41.1 1.1 %pitch2.1 = (f32[8,6,8,512]{3,2,1,0:T(8,128)S(1)}, f32[8,512]{1,0:T(8,128)S(1)}) custom-call(f32[8,6,8,512]{3,2,1,0:T(8,128)S(1)} %get-tuple-element.51.a_ref, f32[8,6,8,128]{3,2,1,0:T(8,128)S(1)} %collective-permute-done.8.prev_ref, f32[8,6,8,128]{3,2,1,0:T(8,128)S(1)} %collective-permute-done.9.next_ref, f32[8,6,8,512]{3,2,1,0:T(8,128)S(1)} %chord2.1.acc_ref, ...), custom_call_target="tpu_custom_call" | custom-call | tf_op jit(solution)/shard_map/pitch2/pallas_call | solution.py:344
  42.3 3.3 %collective-permute-done.14.refs_7_ = f32[8,6,8,128]{3,2,1,0:T(8,128)S(1)} collective-permute-done((f32[8,6,8,128]{3,2,1,0:T(8,128)S(1)}, f32[8,6,8,128]{3,2,1,0:T(8,128)S(1)}, u32[]{:S(2)}, u32[]{:S(2)}) %collective-permute-start.14) | collective-permute-done | bytes 196640 | tf_op jit(solution)/shard_map/ppermute | solution.py:367
  45.7 2.2 %last.1 = (f32[8,6,8,512]{3,2,1,0:T(8,128)S(1)}, f32[32,8,128]{2,1,0:T(8,128)}) custom-call(f32[8,6,8,512]{3,2,1,0:T(8,128)S(1)} %get-tuple-element.56.refs_0_, f32[8,512]{1,0:T(8,128)S(1)} %get-tuple-element.57.refs_1_, f32[8,6,8,512]{3,2,1,0:T(8,128)S(1)} %copy-done, f32[8,512,128]{2,1,0:T(8,128)S(1)} %copy-done.1, s32[8,512]{1,0:T(8,128)S(1)} %copy-done.2, ...), custom_call_target="tpu_custom_call" | custom-call | tf_op jit(solution)/shard_map/last/pallas_call | solution.py:344
  47.9 4.9 %all-to-all-start = ((f32[32,8,128]{2,1,0:T(8,128)}), f32[32,8,128]{2,1,0:T(8,128)S(1)}, u32[]{:S(2)}, u32[]{:S(2)}) async-start(f32[32,8,128]{2,1,0:T(8,128)} %get-tuple-element.63), calls=%async_computation | async-start | bytes 262144 | tf_op jit(solution)/shard_map/all_to_all | solution.py:433
  53.7 7.3 %all-to-all-done = f32[32,8,128]{2,1,0:T(8,128)S(1)} async-done(((f32[32,8,128]{2,1,0:T(8,128)}), f32[32,8,128]{2,1,0:T(8,128)S(1)}, u32[]{:S(2)}, u32[]{:S(2)}) %all-to-all-start) | async-done | bytes 131104 | tf_op jit(solution)/shard_map/all_to_all | solution.py:433
  (27 shorter events, 4.1 us)
Async XLA Ops:
  1.9 12.4 %collective-permute-start.2 = (f32[8,6,8,128]{3,2,1,0:T(8,128)S(1)}, f32[8,6,8,128]{3,2,1,0:T(8,128)S(1)}, u32[]{:S(2)}, u32[]{:S(2)}) collective-permute-start(f32[8,6,8,128]{3,2,1,0:T(8,128)S(1)} %get-tuple-element.44), channel_id=1, source_target_pairs={{0,8},{8,0},{16,24},{24,16},{1,9},{9,1},{17,25},{25,17},{2,10},{10... | collective-permute-start | bytes 589832 | tf_op jit(solution)/shard_map/ppermute | solution.py:367
  5.0 10.6 %collective-permute-start.3 = (f32[8,6,8,128]{3,2,1,0:T(8,128)S(1)}, f32[8,6,8,128]{3,2,1,0:T(8,128)S(1)}, u32[]{:S(2)}, u32[]{:S(2)}) collective-permute-start(f32[8,6,8,128]{3,2,1,0:T(8,128)S(1)} %get-tuple-element.45), channel_id=1, source_target_pairs={{0,16},{8,24},{16,0},{24,8},{1,17},{9,25},{17,1},{25,9},{2,18},{10... | collective-permute-start | bytes 589832 | tf_op jit(solution)/shard_map/ppermute | solution.py:367
  6.5 9.1 %collective-permute-start.4 = (f32[8,6,8,128]{3,2,1,0:T(8,128)S(1)}, f32[8,6,8,128]{3,2,1,0:T(8,128)S(1)}, u32[]{:S(2)}, u32[]{:S(2)}) collective-permute-start(f32[8,6,8,128]{3,2,1,0:T(8,128)S(1)} %get-tuple-element.46), channel_id=1, source_target_pairs={{0,24},{8,16},{16,8},{24,0},{1,25},{9,17},{17,9},{25,1},{2,26},{10... | collective-permute-start | bytes 589832 | tf_op jit(solution)/shard_map/ppermute | solution.py:367
  6.5 13.2 %collective-permute-start = (f32[8,6,8,128]{3,2,1,0:T(8,128)S(1)}, f32[8,6,8,128]{3,2,1,0:T(8,128)S(1)}, u32[]{:S(2)}, u32[]{:S(2)}) collective-permute-start(f32[8,6,8,128]{3,2,1,0:T(8,128)S(1)} %get-tuple-element.34), channel_id=1, source_target_pairs={{0,1},{1,2},{2,3},{3,4},{4,5},{5,6},{6,7},{7,0},{8,9},{9,10},{10,1... | collective-permute-start | bytes 589832 | tf_op jit(solution)/shard_map/ppermute | solution.py:373
  6.5 13.2 %collective-permute-start.1 = (f32[8,6,8,128]{3,2,1,0:T(8,128)S(1)}, f32[8,6,8,128]{3,2,1,0:T(8,128)S(1)}, u32[]{:S(2)}, u32[]{:S(2)}) collective-permute-start(f32[8,6,8,128]{3,2,1,0:T(8,128)S(1)} %get-tuple-element.35), channel_id=1, source_target_pairs={{1,0},{2,1},{3,2},{4,3},{5,4},{6,5},{7,6},{0,7},{9,8},{10,9},{11,1... | collective-permute-start | bytes 589832 | tf_op jit(solution)/shard_map/ppermute | solution.py:374
  16.2 7.7 %collective-permute-start.5 = (f32[8,6,8,128]{3,2,1,0:T(8,128)S(1)}, f32[8,6,8,128]{3,2,1,0:T(8,128)S(1)}, u32[]{:S(2)}, u32[]{:S(2)}) collective-permute-start(f32[8,6,8,128]{3,2,1,0:T(8,128)S(1)} %get-tuple-element.48.refs_6_), channel_id=1, source_target_pairs={{0,8},{8,0},{16,24},{24,16},{1,9},{9,1},{17,25},{25,17},{2,10},{10... | collective-permute-start | bytes 589832 | tf_op jit(solution)/shard_map/ppermute | solution.py:367
  17.5 11.9 %collective-permute-start.6 = (f32[8,6,8,128]{3,2,1,0:T(8,128)S(1)}, f32[8,6,8,128]{3,2,1,0:T(8,128)S(1)}, u32[]{:S(2)}, u32[]{:S(2)}) collective-permute-start(f32[8,6,8,128]{3,2,1,0:T(8,128)S(1)} %get-tuple-element.49.refs_7_), channel_id=1, source_target_pairs={{0,16},{8,24},{16,0},{24,8},{1,17},{9,25},{17,1},{25,9},{2,18},{10... | collective-permute-start | bytes 589832 | tf_op jit(solution)/shard_map/ppermute | solution.py:367
  18.6 10.8 %collective-permute-start.7 = (f32[8,6,8,128]{3,2,1,0:T(8,128)S(1)}, f32[8,6,8,128]{3,2,1,0:T(8,128)S(1)}, u32[]{:S(2)}, u32[]{:S(2)}) collective-permute-start(f32[8,6,8,128]{3,2,1,0:T(8,128)S(1)} %get-tuple-element.50.refs_8_), channel_id=1, source_target_pairs={{0,24},{8,16},{16,8},{24,0},{1,25},{9,17},{17,9},{25,1},{2,26},{10... | collective-permute-start | bytes 589832 | tf_op jit(solution)/shard_map/ppermute | solution.py:367
  21.2 12.1 %collective-permute-start.10 = (f32[8,6,8,128]{3,2,1,0:T(8,128)S(1)}, f32[8,6,8,128]{3,2,1,0:T(8,128)S(1)}, u32[]{:S(2)}, u32[]{:S(2)}) collective-permute-start(f32[8,6,8,128]{3,2,1,0:T(8,128)S(1)} %get-tuple-element.40.refs_1_), channel_id=1, source_target_pairs={{0,8},{8,0},{16,24},{24,16},{1,9},{9,1},{17,25},{25,17},{2,10},{10... | collective-permute-start | bytes 589832 | tf_op jit(solution)/shard_map/ppermute | solution.py:367
  22.5 13.1 %collective-permute-start.11 = (f32[8,6,8,128]{3,2,1,0:T(8,128)S(1)}, f32[8,6,8,128]{3,2,1,0:T(8,128)S(1)}, u32[]{:S(2)}, u32[]{:S(2)}) collective-permute-start(f32[8,6,8,128]{3,2,1,0:T(8,128)S(1)} %get-tuple-element.41.refs_2_), channel_id=1, source_target_pairs={{0,16},{8,24},{16,0},{24,8},{1,17},{9,25},{17,1},{25,9},{2,18},{10... | collective-permute-start | bytes 589832 | tf_op jit(solution)/shard_map/ppermute | solution.py:367
  23.9 11.8 %collective-permute-start.12 = (f32[8,6,8,128]{3,2,1,0:T(8,128)S(1)}, f32[8,6,8,128]{3,2,1,0:T(8,128)S(1)}, u32[]{:S(2)}, u32[]{:S(2)}) collective-permute-start(f32[8,6,8,128]{3,2,1,0:T(8,128)S(1)} %get-tuple-element.42.refs_3_), channel_id=1, source_target_pairs={{0,24},{8,16},{16,8},{24,0},{1,25},{9,17},{17,9},{25,1},{2,26},{10... | collective-permute-start | bytes 589832 | tf_op jit(solution)/shard_map/ppermute | solution.py:367
  29.7 11.5 %copy-start = (f32[8,6,8,512]{3,2,1,0:T(8,128)S(1)}, f32[8,6,8,512]{3,2,1,0:T(8,128)}, u32[]{:S(2)}) copy-start(f32[8,6,8,512]{3,2,1,0:T(8,128)} %refs_2_.1) | copy-start | bytes 2359300
  29.7 11.4 %collective-permute-start.8 = (f32[8,6,8,128]{3,2,1,0:T(8,128)S(1)}, f32[8,6,8,128]{3,2,1,0:T(8,128)S(1)}, u32[]{:S(2)}, u32[]{:S(2)}) collective-permute-start(f32[8,6,8,128]{3,2,1,0:T(8,128)S(1)} %get-tuple-element.52), channel_id=1, source_target_pairs={{0,1},{1,2},{2,3},{3,4},{4,5},{5,6},{6,7},{7,0},{8,9},{9,10},{10,1... | collective-permute-start | bytes 589832 | tf_op jit(solution)/shard_map/ppermute | solution.py:373
  29.7 11.4 %collective-permute-start.9 = (f32[8,6,8,128]{3,2,1,0:T(8,128)S(1)}, f32[8,6,8,128]{3,2,1,0:T(8,128)S(1)}, u32[]{:S(2)}, u32[]{:S(2)}) collective-permute-start(f32[8,6,8,128]{3,2,1,0:T(8,128)S(1)} %get-tuple-element.53), channel_id=1, source_target_pairs={{1,0},{2,1},{3,2},{4,3},{5,4},{6,5},{7,6},{0,7},{9,8},{10,9},{11,1... | collective-permute-start | bytes 589832 | tf_op jit(solution)/shard_map/ppermute | solution.py:374
  36.3 6.0 %collective-permute-start.13 = (f32[8,6,8,128]{3,2,1,0:T(8,128)S(1)}, f32[8,6,8,128]{3,2,1,0:T(8,128)S(1)}, u32[]{:S(2)}, u32[]{:S(2)}) collective-permute-start(f32[8,6,8,128]{3,2,1,0:T(8,128)S(1)} %get-tuple-element.59), channel_id=1, source_target_pairs={{0,8},{8,0},{16,24},{24,16},{1,9},{9,1},{17,25},{25,17},{2,10},{10... | collective-permute-start | bytes 589832 | tf_op jit(solution)/shard_map/ppermute | solution.py:367
  37.0 8.7 %collective-permute-start.14 = (f32[8,6,8,128]{3,2,1,0:T(8,128)S(1)}, f32[8,6,8,128]{3,2,1,0:T(8,128)S(1)}, u32[]{:S(2)}, u32[]{:S(2)}) collective-permute-start(f32[8,6,8,128]{3,2,1,0:T(8,128)S(1)} %get-tuple-element.60), channel_id=1, source_target_pairs={{0,16},{8,24},{16,0},{24,8},{1,17},{9,25},{17,1},{25,9},{2,18},{10... | collective-permute-start | bytes 589832 | tf_op jit(solution)/shard_map/ppermute | solution.py:367
  38.6 7.1 %collective-permute-start.15 = (f32[8,6,8,128]{3,2,1,0:T(8,128)S(1)}, f32[8,6,8,128]{3,2,1,0:T(8,128)S(1)}, u32[]{:S(2)}, u32[]{:S(2)}) collective-permute-start(f32[8,6,8,128]{3,2,1,0:T(8,128)S(1)} %get-tuple-element.61), channel_id=1, source_target_pairs={{0,24},{8,16},{16,8},{24,0},{1,25},{9,17},{17,9},{25,1},{2,26},{10... | collective-permute-start | bytes 589832 | tf_op jit(solution)/shard_map/ppermute | solution.py:367
  41.1 4.6 %copy-start.1 = (f32[8,512,128]{2,1,0:T(8,128)S(1)}, f32[8,512,128]{2,1,0:T(8,128)}, u32[]{:S(2)}) copy-start(f32[8,512,128]{2,1,0:T(8,128)} %refs_3_.1) | copy-start | bytes 6291460
  41.1 4.6 %copy-start.2 = (s32[8,512]{1,0:T(8,128)S(1)}, s32[8,512]{1,0:T(8,128)}, u32[]{:S(2)}) copy-start(s32[8,512]{1,0:T(8,128)} %refs_4_.1) | copy-start | bytes 49156
  47.9 13.1 %all-to-all-start = ((f32[32,8,128]{2,1,0:T(8,128)}), f32[32,8,128]{2,1,0:T(8,128)S(1)}, u32[]{:S(2)}, u32[]{:S(2)}) async-start(f32[32,8,128]{2,1,0:T(8,128)} %get-tuple-element.63), calls=%async_computation | async-start | bytes 262144 | tf_op jit(solution)/shard_map/all_to_all | solution.py:433

commit v3 on v2

--- a/solution.py
+++ b/solution.py
@@ -84,7 +84,7 @@
 
 
 def pack_kernel(n_inst, a_hbm, a_ref, *refs):
-    chunks, (first_ref, last_ref, arrived) = refs[:n_inst], refs[n_inst:]
+    chunks, (arrived,) = refs[:n_inst], refs[n_inst:]
     steps, nv, _, ny = a_ref.shape
     me = lax.axis_index("inst")
 
@@ -100,10 +100,17 @@
             y, k0 = chunk_place(me ^ r, n_inst, nv, ny)
             for k in range(chunks[0].shape[1]):
                 chunks[r][t, k] = a_ref[t, k0 + k, :, lane_tile(y)]
+        return 0
+
+    lax.fori_loop(0, steps, at_step, 0)
+
+
+def edges_kernel(a_ref, first_ref, last_ref):
+    def at_step(t, _):
         pack_edges(t, a_ref, first_ref, last_ref)
         return 0
 
-    lax.fori_loop(0, steps, at_step, 0)
+    lax.fori_loop(0, a_ref.shape[0], at_step, 0)
 
 
 def pack_edges(t, a_ref, first_ref, last_ref):
@@ -134,12 +141,10 @@
 
 
 def first_chord_kernel(
-    a_ref, src_hbm, d_hbm, fx_hbm, fy_hbm,
-    acc_ref, src_ref, inverse, fx_ref, fy_ref, chord, d_ref, arrived, d_arrived,
+    a_ref, src_hbm, d_hbm, fy_hbm, acc_ref, src_ref, inverse, fy_ref, chord, d_ref, arrived, d_arrived
 ):
     steps = a_ref.shape[0]
-
-    pairs = ((src_hbm, src_ref), (fy_hbm, fy_ref), (fx_hbm, fx_ref))
+    pairs = ((src_hbm, src_ref), (fy_hbm, fy_ref))
 
     def copy(i, t):
         there, here = pairs[i]
@@ -150,8 +155,6 @@
         copy(0, t).start()
         copy(1, t).start()
     d_copy.start()
-    for t in range(steps):
-        copy(2, t).start()
 
     def at_step(t, _):
         copy(0, t).wait()
@@ -162,8 +165,6 @@
     lax.fori_loop(0, steps, at_step, 0)
     d_copy.wait()
     inverse[...] = 1.0 / d_ref[...]
-    for t in range(steps):
-        copy(2, t).wait()
 
 
 def second_chord_kernel(a_ref, src_ref, fy_ref, acc_ref, chord):
@@ -203,14 +204,21 @@
     return total * inverse[k, :, lanes]
 
 
-def first_pitch_kernel(n_inst, a_ref, prev_ref, next_ref, acc_ref, fx_ref, inverse, *refs):
-    out_refs, (pitch, near) = refs[:n_inst], refs[n_inst:]
+def first_pitch_kernel(n_inst, a_ref, prev_ref, next_ref, acc_ref, fx_hbm, inverse, *refs):
+    out_refs, (fx_ref, pitch, near, arrived) = refs[:n_inst], refs[n_inst:]
     nv, _, ny = pitch.shape
     part = out_refs[0].shape[1]
     me = lax.axis_index("inst")
 
+    def copy(t):
+        return pltpu.make_async_copy(fx_hbm.at[t], fx_ref.at[t], arrived.at[t])
+
+    for t in range(a_ref.shape[0]):
+        copy(t).start()
+
     def at_step(t, _):
         pitch_terms(t, a_ref, prev_ref, next_ref, pitch, near)
+        copy(t).wait()
         for r in range(n_inst):
             y, k0 = chunk_place(me ^ r, n_inst, nv, ny)
             lanes = lane_tile(y)
@@ -225,10 +233,8 @@
 
 
 def spectral_kernel(n_inst, second, inverse, *refs):
-    in_refs = refs[:n_inst]
-    shift_refs = refs[n_inst : 2 * n_inst] if second else ()
-    out_refs = refs[(2 if second else 1) * n_inst : (3 if second else 2) * n_inst]
-    (work,) = refs[(3 if second else 2) * n_inst :]
+    in_refs, shift_refs = refs[:n_inst], refs[n_inst : 2 * n_inst]
+    out_refs, (work,) = refs[2 * n_inst : 3 * n_inst], refs[3 * n_inst :]
     per, part = in_refs[0].shape[:2]
     nv, _, ny = inverse.shape
     me = lax.axis_index("inst")
@@ -257,7 +263,7 @@
 
 def join_kernel(n_inst, *refs):
     b_refs, z_refs = refs[:n_inst], refs[n_inst : 2 * n_inst]
-    a_ref, first_ref, last_ref = refs[2 * n_inst :]
+    a_ref, first_ref, last_ref = refs[-3:]
     steps, nv, _, ny = a_ref.shape
     me = lax.axis_index("inst")
 
@@ -294,63 +300,122 @@
     lax.fori_loop(0, a_ref.shape[0], at_step, 0)
 
 
-def last_kernel(n_inst, x_ref, weight_ref, shape_ref, mode_ref, patch_ref, *refs):
-    z_refs, (a_ref, send_ref, weight) = refs[:n_inst], refs[n_inst:]
-    steps, nv, rows, ny = x_ref.shape
-    part = z_refs[0].shape[1]
+def basis_kernel(mode_ref, _, split_ref):
+    def at_row(x, _):
+        mode = mode_ref[x]
+        high = mode.astype(jnp.bfloat16)
+        split_ref[x, :, :LANES] = high
+        split_ref[x, :, LANES:] = (mode - high.astype(F32)).astype(jnp.bfloat16)
+        return 0
+
+    lax.fori_loop(0, mode_ref.shape[0], at_row, 0)
+
+
+def weight_kernel(n_inst, x_weight_ref, shape_ref, *refs):
+    z_refs, (weight,) = refs[:n_inst], refs[n_inst:]
+    steps, nv, _, ny = shape_ref.shape
+    me = lax.axis_index("inst")
+    weight[...] = x_weight_ref[...]
+    for r in range(n_inst):
+        y, k0 = chunk_place(me ^ r, n_inst, nv, ny)
+        lanes = lane_tile(y)
+
+        def at_step(t, total):
+            for k in range(z_refs[0].shape[1]):
+                total = total - z_refs[r][t, k] * shape_ref[t, k0 + k, :, lanes]
+            return total
+
+        weight[:, lanes] = lax.fori_loop(0, steps, at_step, weight[:, lanes])
+
+
+def own_block(inst, space, n_inst, n_space, choose):
+    first = n_inst * space
+    apart = inst ^ (first // n_space)
+    to_first = abs(first % n_space - space)
+    to_last = abs(first % n_space + n_inst - 1 - space)
+    return choose(to_first >= to_last, apart, n_inst - 1 - apart)
+
+
+def sums_kernel(n_inst, n_space, split_ref, patch_ref, *refs):
+    weight_refs, (block_ref, beyond_ref, blocks) = refs[:n_inst], refs[n_inst:]
+    rows, ny = patch_ref.shape
     me, space = lax.axis_index("inst"), lax.axis_index("space")
-    owners = send_ref.shape[0]
+    over = REACH // PATCH_DEV
     per_space = PATCH_DEV * n_inst
     window = per_space + 2 * REACH
-    weight[...] = weight_ref[...]
+    weight = weight_refs[0][...]
+    for other in weight_refs[1:]:
+        weight = weight + other[...]
+    ids = lax.broadcasted_iota(jnp.int32, (window, ny), 0) + (per_space * space - REACH)
+    acc = jnp.zeros((window, LANES), F32)
+    for x in range(rows):
+        row = weight[x : x + 1, :]
+        high = row.astype(jnp.bfloat16).astype(F32)
+        hit = ids == patch_ref[x : x + 1, :]
+        factors = jnp.concatenate(
+            [
+                jnp.where(hit, high, 0.0).astype(jnp.bfloat16),
+                jnp.where(hit, row - high, 0.0).astype(jnp.bfloat16),
+            ],
+            axis=0,
+        )
+        product = jnp.dot(factors, split_ref[x], preferred_element_type=F32)
+        acc = acc + (
+            (product[:window, :LANES] + product[window:, :LANES])
+            + (product[:window, LANES:] + product[window:, LANES:])
+        )
+    for j in range(window // PATCH_DEV):
+        blocks[j] = acc[j * PATCH_DEV : (j + 1) * PATCH_DEV]
+    block_ref[...] = blocks[over + own_block(me, space, n_inst, n_space, jnp.where)]
+    side = jnp.minimum(me, 2 * over - 1)
+    beyond_ref[...] = blocks[jnp.where(side < over, side, side + n_inst)]
+
+
+def adjoint_kernel(n_inst, x_ref, _, *refs):
+    z_refs, (out_hbm, a_ref, left) = refs[:n_inst], refs[n_inst:]
+    steps, nv, _, ny = x_ref.shape
+    me = lax.axis_index("inst")
+
+    def copy(t):
+        return pltpu.make_async_copy(a_ref.at[t], out_hbm.at[t], left.at[t])
 
     def at_step(t, _):
         for r in range(n_inst):
             y, k0 = chunk_place(me ^ r, n_inst, nv, ny)
-            total = jnp.zeros((rows, LANES), F32)
-            for k in range(part):
-                z = z_refs[r][t, k]
+            for k in range(z_refs[0].shape[1]):
                 a_ref[t, k0 + k, :, lane_tile(y)] = (
-                    x_ref[t, k0 + k, :, lane_tile(y)] - z
+                    x_ref[t, k0 + k, :, lane_tile(y)] - z_refs[r][t, k]
                 )
-                total = total + z * shape_ref[t, k0 + k, :, lane_tile(y)]
-            weight[:, lane_tile(y)] = weight[:, lane_tile(y)] - total
+        copy(t).start()
         return 0
 
     lax.fori_loop(0, steps, at_step, 0)
-    first = per_space * space - REACH
-    ids = lax.broadcasted_iota(jnp.int32, (window, ny), 0) + first
-    acc = jnp.zeros((window, LANES), F32)
-    for x in range(rows):
-        hit = jnp.where(ids == patch_ref[x : x + 1, :], weight[x : x + 1, :], 0.0)
-        acc = acc + jnp.dot(
-            hit, mode_ref[x], precision=lax.Precision.HIGHEST, preferred_element_type=F32
-        )
-    send_ref[...] = jnp.zeros_like(send_ref)
-    first_owner = n_inst * space - REACH // PATCH_DEV
-    for j in range(window // PATCH_DEV):
-        owner = first_owner + j
-
-        @pl.when((owner >= 0) & (owner < owners))
-        def _():
-            send_ref[owner] = acc[j * PATCH_DEV : (j + 1) * PATCH_DEV]
-
-
-def call(kernel, outs, scratch=(), n_hbm=None, name=None):
+    for t in range(steps):
+        copy(t).wait()
+
+
+def total_kernel(block_ref, beyond_ref, out_ref):
+    out_ref[...] = block_ref[...] + beyond_ref[...]
+
+
+def call(kernel, outs, scratch=(), n_hbm=None):
     n_hbm = n_hbm or ()
     scratch_shapes = [pltpu.VMEM(x, F32) if isinstance(x, tuple) else x for x in scratch]
 
     def run(*args):
         return pl.pallas_call(
             kernel,
-            out_shape=[pltpu.VMEM(shape, F32) for shape in outs],
+            out_shape=[pltpu.VMEM(x, F32) if isinstance(x, tuple) else x for x in outs],
+            out_specs=[
+                pl.BlockSpec(memory_space=pltpu.VMEM if isinstance(x, tuple) else x.memory_space)
+                for x in outs
+            ],
             in_specs=[
                 pl.BlockSpec(memory_space=pltpu.HBM if i in n_hbm else pltpu.VMEM)
                 for i in range(len(args))
             ],
             scratch_shapes=scratch_shapes,
             compiler_params=pltpu.CompilerParams(vmem_limit_bytes=SCRATCH_LIMIT),
-            name=name,
         )(
             *(
                 pltpu.with_memory_space_constraint(x, pltpu.HBM if i in n_hbm else pltpu.VMEM)
@@ -361,6 +426,23 @@
     return run
 
 
+def owner_pairs(n_inst, n_space):
+    own, beyond = [], []
+    over = REACH // PATCH_DEV
+    for inst in range(n_inst):
+        for space in range(n_space):
+            here, first = inst * n_space + space, n_inst * space
+            block = own_block(
+                inst, space, n_inst, n_space, lambda test, yes, no: yes if test else no
+            )
+            own.append((here, first + block))
+            if inst < 2 * over:
+                owner = first + (inst - over if inst < over else n_inst + inst - over)
+                if 0 <= owner < n_inst * n_space:
+                    beyond.append((here, owner))
+    return own, beyond
+
+
 def make_body(n_inst, n_space):
     def exchange(chunks):
         return [chunks[0]] + [
@@ -387,51 +469,58 @@
 
             return run
 
-        a0, *chunks, first, last = call(
-            bound(pack_kernel, n_inst), [start.shape] + [chunk] * n_inst + [edge] * 2,
-            scratch=[pltpu.SemaphoreType.DMA((steps,))], n_hbm=(0,), name="pack",
+        a0, *chunks = call(
+            bound(pack_kernel, n_inst), [start.shape] + [chunk] * n_inst,
+            scratch=[pltpu.SemaphoreType.DMA((steps,))], n_hbm=(0,),
         )(start)
+        start_cells = exchange(chunks)
+        first, last = call(edges_kernel, [edge, edge])(a0)
         before, after = edges(first, last)
-        start_cells = exchange(chunks)
-        acc, src, inverse, fx, fy = call(
-            first_chord_kernel,
-            [start.shape, source.shape, tile, flux_x.shape, flux_y.shape],
+        acc, src, inverse, fy = call(
+            first_chord_kernel, [start.shape, source.shape, tile, flux_y.shape],
             scratch=[
-                tile, tile, pltpu.SemaphoreType.DMA((3, steps)), pltpu.SemaphoreType.DMA(())
+                tile, tile, pltpu.SemaphoreType.DMA((2, steps)), pltpu.SemaphoreType.DMA(())
             ],
-            n_hbm=(1, 2, 3, 4), name="chord1",
-        )(a0, source, diagonal, flux_x, flux_y)
-        b = call(
-            bound(first_pitch_kernel, n_inst), [chunk] * n_inst, scratch=[tile, tile], name="pitch1"
-        )(a0, before, after, acc, fx, inverse)
+            n_hbm=(1, 2, 3),
+        )(a0, source, diagonal, flux_y)
+        *b, fx = call(
+            bound(first_pitch_kernel, n_inst), [chunk] * n_inst + [flux_x.shape],
+            scratch=[tile, tile, pltpu.SemaphoreType.DMA((steps,))], n_hbm=(4,),
+        )(a0, before, after, acc, flux_x, inverse)
         b_cells = exchange(b)
         z0_cells = call(
             bound(spectral_kernel, n_inst, False), [chunk] * n_inst, scratch=[(NT, 8, LANES)],
-            name="spectral1",
-        )(inverse, *start_cells)
+        )(inverse, *start_cells, *([acc] * n_inst))
         z0 = exchange(z0_cells)
         z1_cells = call(
             bound(spectral_kernel, n_inst, True), [chunk] * n_inst, scratch=[(NT, 8, LANES)],
-            name="spectral2",
         )(inverse, *b_cells, *z0_cells)
         z1 = exchange(z1_cells)
-        a1, first, last = call(
-            bound(join_kernel, n_inst), [start.shape, edge, edge], name="join"
-        )(*b, *z0)
+        a1, first, last = call(bound(join_kernel, n_inst), [start.shape, edge, edge])(*b, *z0)
         before, after = edges(first, last)
-        (acc,) = call(second_chord_kernel, [start.shape], scratch=[tile], name="chord2")(
-            a1, src, fy
+        (acc,) = call(second_chord_kernel, [start.shape], scratch=[tile])(a1, src, fy)
+        x, weight = call(
+            second_pitch_kernel, [start.shape, (rows, ny)], scratch=[tile, tile]
+        )(a1, before, after, acc, fx, inverse, shape_derivative)
+        (split,) = call(
+            basis_kernel, [pltpu.VMEM((rows, ny, 2 * LANES), jnp.bfloat16)]
+        )(mode_basis, weight)
+        (weight,) = call(bound(weight_kernel, n_inst), [(rows, ny)])(weight, shape_derivative, *z1)
+        weights = exchange([weight] * n_inst)
+        block, beyond = call(
+            bound(sums_kernel, n_inst, n_space), [(PATCH_DEV, LANES)] * 2,
+            scratch=[(n_inst + 2 * REACH // PATCH_DEV, PATCH_DEV, LANES)],
+        )(split, patch_of_cell, *weights)
+        block, beyond = (
+            lax.ppermute(x, ("inst", "space"), pairs)
+            for x, pairs in zip((block, beyond), owner_pairs(n_inst, n_space))
         )
-        x, weight = call(
-            second_pitch_kernel, [start.shape, (rows, ny)], scratch=[tile, tile], name="pitch2"
-        )(a1, before, after, acc, fx, inverse, shape_derivative)
-        owners = n_inst * n_space
-        adjoint, sends = call(
-            bound(last_kernel, n_inst), [start.shape, (owners, PATCH_DEV, LANES)],
-            scratch=[(rows, ny)], name="last",
-        )(x, weight, shape_derivative, mode_basis, patch_of_cell, *z1)
-        parts = lax.all_to_all(sends, ("inst", "space"), 0, 0, tiled=True)
-        return adjoint, jnp.sum(parts, axis=0)
+        (adjoint,) = call(
+            bound(adjoint_kernel, n_inst), [pltpu.HBM(start.shape, F32)],
+            scratch=[start.shape, pltpu.SemaphoreType.DMA((steps,))],
+        )(x, weight, *z1)
+        (sensitivity,) = call(total_kernel, [(PATCH_DEV, LANES)])(block, beyond)
+        return adjoint, sensitivity
 
     return body
 
@@ -447,8 +536,12 @@
         P("space", None, None),
         P("space", None),
     )
+    n_inst, n_space = mesh.shape["inst"], mesh.shape["space"]
+    body = make_body(n_inst, n_space)
+
+
     return jax.shard_map(
-        make_body(mesh.shape["inst"], mesh.shape["space"]),
+        body,
         mesh=mesh,
         in_specs=placed,
         out_specs=(P("inst", None, "space", None), P(("inst", "space"), None)),

time: 61.8 us -> 61.6 us (level)
  the two profiles are of different devices: /device:TPU:0 before, /device:TPU:9 now
where the time goes in v3:
time: 61.6 us; the launch traced here: 61.4 us
  starting transfers between devices  34.3 us (56%)
  Pallas kernels  12.9 us (21%)
  waiting for transfers between devices  12.8 us (21%)
  between operations  0.82 us (1%)
    ppermute x15, starting transfers between devices, exchange(): lax.ppermute(chunks[r], 'inst', [(i, i ^ r) for i in range(n_inst)])  13.6 us
    pallas_call x14, Pallas kernels, run(): pl.pallas_call(kernel, out_shape=[pltpu.VMEM(x, F32) if isinstance(x, tup...  12.9 us
    ppermute x2, starting transfers between devices, body(): lax.ppermute(x, ('inst', 'space'), pairs)  10.8 us
    ppermute x15, waiting for transfers between devices, exchange(): lax.ppermute(chunks[r], 'inst', [(i, i ^ r) for i in range(n_inst)])  10.3 us
    ppermute x2, starting transfers between devices, edges(): before = lax.ppermute(last, 'space', ring)  9.9 us
    ppermute x2, waiting for transfers between devices, body(): lax.ppermute(x, ('inst', 'space'), pairs)  2.34 us
  transfers between devices with their start and end apart: 21, of which 9 were waited for; matrix products, arithmetic and copies ran while one was open for 0% of the time, Pallas kernels for 18%

profile of v3, /device:TPU:9, one launch (start us, length us, event | category | flops | bytes accessed | tf_op | source)
XLA Modules:
  0.0 61.4 jit_solution(18201864244612589208)
XLA Ops:
  0.6 1.3 %shard_map.95 = (f32[8,6,8,512]{3,2,1,0:T(8,128)S(1)}, f32[8,6,8,128]{3,2,1,0:T(8,128)S(1)}, f32[8,6,8,128]{3,2,1,0:T(8,128)S(1)}, f32[8,6,8,128]{3,2,1,0:T(8,128)S(1)}, f32[8,6,8,128]{3,2,1,0:T(8,128)S(1)}) custom-call(f32[8,6,8,512]{3,2,1,0:T(8,128)} %refs_0_.1), custom_call_target="tpu_custom_call" | custom-call | tf_op jit(solution)/shard_map/pallas_call | solution.py:406
  1.9 1.3 %collective-permute-start.2 = (f32[8,6,8,128]{3,2,1,0:T(8,128)S(1)}, f32[8,6,8,128]{3,2,1,0:T(8,128)S(1)}, u32[]{:S(2)}, u32[]{:S(2)}) collective-permute-start(f32[8,6,8,128]{3,2,1,0:T(8,128)S(1)} %get-tuple-element.43), channel_id=1, source_target_pairs={{0,8},{8,0},{16,24},{24,16},{1,9},{9,1},{17,25},{25,17},{2,10},{10... | collective-permute-start | bytes 589832 | tf_op jit(solution)/shard_map/ppermute | solution.py:449
  3.2 1.2 %collective-permute-start.3 = (f32[8,6,8,128]{3,2,1,0:T(8,128)S(1)}, f32[8,6,8,128]{3,2,1,0:T(8,128)S(1)}, u32[]{:S(2)}, u32[]{:S(2)}) collective-permute-start(f32[8,6,8,128]{3,2,1,0:T(8,128)S(1)} %get-tuple-element.44), channel_id=1, source_target_pairs={{0,16},{8,24},{16,0},{24,8},{1,17},{9,25},{17,1},{25,9},{2,18},{10... | collective-permute-start | bytes 589832 | tf_op jit(solution)/shard_map/ppermute | solution.py:449
  4.8 2.7 %collective-permute-start = (f32[8,6,8,128]{3,2,1,0:T(8,128)S(1)}, f32[8,6,8,128]{3,2,1,0:T(8,128)S(1)}, u32[]{:S(2)}, u32[]{:S(2)}) collective-permute-start(f32[8,6,8,128]{3,2,1,0:T(8,128)S(1)} %get-tuple-element.34), channel_id=1, source_target_pairs={{0,1},{1,2},{2,3},{3,4},{4,5},{5,6},{6,7},{7,0},{8,9},{9,10},{10,1... | collective-permute-start | bytes 589832 | tf_op jit(solution)/shard_map/ppermute | solution.py:455
  7.5 2.9 %shard_map.97 = (f32[8,6,8,512]{3,2,1,0:T(8,128)S(1)}, f32[8,6,8,512]{3,2,1,0:T(8,128)S(1)}, f32[6,8,512]{2,1,0:T(8,128)S(1)}, f32[8,6,6,8,512]{4,3,2,1,0:T(8,128)S(1)}) custom-call(f32[8,6,8,512]{3,2,1,0:T(8,128)S(1)} %get-tuple-element.33.a_ref.refs_0_, f32[8,6,8,512]{3,2,1,0:T(8,128)} %src_hbm.1, f32[6,8,512]{2,1,0:T(8,128)} %d_hbm.1, ...), custom_call_target="tpu_custom_call" | custom-call | tf_op jit(solution)/shard_map/pallas_call | solution.py:406
  10.4 2.6 %collective-permute-done.4.refs_4_ = f32[8,6,8,128]{3,2,1,0:T(8,128)S(1)} collective-permute-done((f32[8,6,8,128]{3,2,1,0:T(8,128)S(1)}, f32[8,6,8,128]{3,2,1,0:T(8,128)S(1)}, u32[]{:S(2)}, u32[]{:S(2)}) %collective-permute-start.4) | collective-permute-done | bytes 196640 | tf_op jit(solution)/shard_map/ppermute | solution.py:449
  13.6 1.2 %collective-permute-start.5 = (f32[8,6,8,128]{3,2,1,0:T(8,128)S(1)}, f32[8,6,8,128]{3,2,1,0:T(8,128)S(1)}, u32[]{:S(2)}, u32[]{:S(2)}) collective-permute-start(f32[8,6,8,128]{3,2,1,0:T(8,128)S(1)} %get-tuple-element.47.refs_6_), channel_id=1, source_target_pairs={{0,8},{8,0},{16,24},{24,16},{1,9},{9,1},{17,25},{25,17},{2,10},{10... | collective-permute-start | bytes 589832 | tf_op jit(solution)/shard_map/ppermute | solution.py:449
  15.2 1.2 %collective-permute-start.7 = (f32[8,6,8,128]{3,2,1,0:T(8,128)S(1)}, f32[8,6,8,128]{3,2,1,0:T(8,128)S(1)}, u32[]{:S(2)}, u32[]{:S(2)}) collective-permute-start(f32[8,6,8,128]{3,2,1,0:T(8,128)S(1)} %get-tuple-element.49.refs_8_), channel_id=1, source_target_pairs={{0,24},{8,16},{16,8},{24,0},{1,25},{9,17},{17,9},{25,1},{2,26},{10... | collective-permute-start | bytes 589832 | tf_op jit(solution)/shard_map/ppermute | solution.py:449
  16.4 2.6 %shard_map.98 = (f32[8,6,8,128]{3,2,1,0:T(8,128)S(1)}, f32[8,6,8,128]{3,2,1,0:T(8,128)S(1)}, f32[8,6,8,128]{3,2,1,0:T(8,128)S(1)}, f32[8,6,8,128]{3,2,1,0:T(8,128)S(1)}, f32[8,6,6,8,512]{4,3,2,1,0:T(8,128)S(1)}) custom-call(f32[8,6,8,512]{3,2,1,0:T(8,128)S(1)} %get-tuple-element.33.a_ref.refs_0_, f32[8,6,8,128]{3,2,1,0:T(8,128)S(1)} %collective-permute-done.refs_1_, ...), custom_call_target="tpu_custom_call" | custom-call | tf_op jit(solution)/shard_map/pallas_call | solution.py:406
  19.0 1.2 %collective-permute-start.10 = (f32[8,6,8,128]{3,2,1,0:T(8,128)S(1)}, f32[8,6,8,128]{3,2,1,0:T(8,128)S(1)}, u32[]{:S(2)}, u32[]{:S(2)}) collective-permute-start(f32[8,6,8,128]{3,2,1,0:T(8,128)S(1)} %get-tuple-element.39.refs_1_), channel_id=1, source_target_pairs={{0,8},{8,0},{16,24},{24,16},{1,9},{9,1},{17,25},{25,17},{2,10},{10... | collective-permute-start | bytes 589832 | tf_op jit(solution)/shard_map/ppermute | solution.py:449
  20.5 1.2 %collective-permute-start.12 = (f32[8,6,8,128]{3,2,1,0:T(8,128)S(1)}, f32[8,6,8,128]{3,2,1,0:T(8,128)S(1)}, u32[]{:S(2)}, u32[]{:S(2)}) collective-permute-start(f32[8,6,8,128]{3,2,1,0:T(8,128)S(1)} %get-tuple-element.41.refs_3_), channel_id=1, source_target_pairs={{0,24},{8,16},{16,8},{24,0},{1,25},{9,17},{17,9},{25,1},{2,26},{10... | collective-permute-start | bytes 589832 | tf_op jit(solution)/shard_map/ppermute | solution.py:449
  22.8 7.1 %collective-permute-start.8 = (f32[8,6,8,128]{3,2,1,0:T(8,128)S(1)}, f32[8,6,8,128]{3,2,1,0:T(8,128)S(1)}, u32[]{:S(2)}, u32[]{:S(2)}) collective-permute-start(f32[8,6,8,128]{3,2,1,0:T(8,128)S(1)} %get-tuple-element.51), channel_id=1, source_target_pairs={{0,1},{1,2},{2,3},{3,4},{4,5},{5,6},{6,7},{7,0},{8,9},{9,10},{10,1... | collective-permute-start | bytes 589832 | tf_op jit(solution)/shard_map/ppermute | solution.py:455
  30.0 1.3 %collective-permute-done.11.refs_3_ = f32[8,6,8,128]{3,2,1,0:T(8,128)S(1)} collective-permute-done((f32[8,6,8,128]{3,2,1,0:T(8,128)S(1)}, f32[8,6,8,128]{3,2,1,0:T(8,128)S(1)}, u32[]{:S(2)}, u32[]{:S(2)}) %collective-permute-start.11) | collective-permute-done | bytes 196640 | tf_op jit(solution)/shard_map/ppermute | solution.py:449
  32.7 1.8 %collective-permute-start.14 = (f32[8,6,8,128]{3,2,1,0:T(8,128)S(1)}, f32[8,6,8,128]{3,2,1,0:T(8,128)S(1)}, u32[]{:S(2)}, u32[]{:S(2)}) collective-permute-start(f32[8,6,8,128]{3,2,1,0:T(8,128)S(1)} %get-tuple-element.60), channel_id=1, source_target_pairs={{0,16},{8,24},{16,0},{24,8},{1,17},{9,25},{17,1},{25,9},{2,18},{10... | collective-permute-start | bytes 589832 | tf_op jit(solution)/shard_map/ppermute | solution.py:449
  34.7 1.2 %shard_map.101.acc_ref = f32[8,6,8,512]{3,2,1,0:T(8,128)S(1)} custom-call(f32[8,6,8,512]{3,2,1,0:T(8,128)S(1)} %get-tuple-element.50.a_ref, f32[8,6,8,512]{3,2,1,0:T(8,128)S(1)} %get-tuple-element.53.src_ref, f32[8,6,6,8,512]{4,3,2,1,0:T(8,128)S(1)} %get-tuple-element.54.fy_ref), custom_call_target="tpu_custom_call" | custom-call | tf_op jit(solution)/shard_map/pallas_call | solution.py:406
  36.1 1.1 %shard_map.102 = (f32[8,6,8,512]{3,2,1,0:T(8,128)S(1)}, f32[8,512]{1,0:T(8,128)S(1)}) custom-call(f32[8,6,8,512]{3,2,1,0:T(8,128)S(1)} %get-tuple-element.50.a_ref, f32[8,6,8,128]{3,2,1,0:T(8,128)S(1)} %collective-permute-done.8.prev_ref, f32[8,6,8,128]{3,2,1,0:T(8,128)S(1)} %collective-permute-done.9.next_ref, f32[8,6,8,512]{3,2,1,0:T(8,128)S(1)} %shard_map.101.acc_ref, ...), custom_call_target="tpu_custom_call" | custom-call | tf_op jit(solution)/shard_map/pallas_call | solution.py:406
  37.2 2.6 %collective-permute-done.14.refs_4_ = f32[8,6,8,128]{3,2,1,0:T(8,128)S(1)} collective-permute-done((f32[8,6,8,128]{3,2,1,0:T(8,128)S(1)}, f32[8,6,8,128]{3,2,1,0:T(8,128)S(1)}, u32[]{:S(2)}, u32[]{:S(2)}) %collective-permute-start.14) | collective-permute-done | bytes 196640 | tf_op jit(solution)/shard_map/ppermute | solution.py:449
  39.8 1.2 %collective-permute-done.15.refs_5_ = f32[8,6,8,128]{3,2,1,0:T(8,128)S(1)} collective-permute-done((f32[8,6,8,128]{3,2,1,0:T(8,128)S(1)}, f32[8,6,8,128]{3,2,1,0:T(8,128)S(1)}, u32[]{:S(2)}, u32[]{:S(2)}) %collective-permute-start.15) | collective-permute-done | bytes 196640 | tf_op jit(solution)/shard_map/ppermute | solution.py:449
  42.7 1.3 %collective-permute-start.18 = (f32[8,512]{1,0:T(8,128)S(1)}, f32[8,512]{1,0:T(8,128)S(1)}, u32[]{:S(2)}, u32[]{:S(2)}) collective-permute-start(f32[8,512]{1,0:T(8,128)S(1)} %shard_map.104.refs_1_.refs_2_), channel_id=1, source_target_pairs={{0,24},{8,16},{16,8},{24,0},{1,25},{9,17},{17,9},{25,1},{2,26},{10... | collective-permute-start | bytes 49160 | tf_op jit(solution)/shard_map/ppermute | solution.py:449
  44.7 1.5 %collective-permute-done.18.refs_5_ = f32[8,512]{1,0:T(8,128)S(1)} collective-permute-done((f32[8,512]{1,0:T(8,128)S(1)}, f32[8,512]{1,0:T(8,128)S(1)}, u32[]{:S(2)}, u32[]{:S(2)}) %collective-permute-start.18) | collective-permute-done | bytes 16416 | tf_op jit(solution)/shard_map/ppermute | solution.py:449
  46.7 8.9 %collective-permute-start.19 = (f32[8,128]{1,0:T(8,128)S(1)}, f32[8,128]{1,0:T(8,128)S(1)}, u32[]{:S(2)}, u32[]{:S(2)}) collective-permute-start(f32[8,128]{1,0:T(8,128)S(1)} %get-tuple-element.62), channel_id=1, source_target_pairs={{0,3},{1,7},{2,9},{3,14},{4,18},{5,21},{6,27},{7,31},{8,2},{9,6},{... | collective-permute-start | bytes 12296 | tf_op jit(solution)/shard_map/ppermute | solution.py:515
  55.6 1.9 %collective-permute-start.20 = (f32[8,128]{1,0:T(8,128)S(1)}, f32[8,128]{1,0:T(8,128)S(1)}, u32[]{:S(2)}, u32[]{:S(2)}) collective-permute-start(f32[8,128]{1,0:T(8,128)S(1)} %get-tuple-element.63), channel_id=1, source_target_pairs={{1,2},{2,6},{3,10},{4,14},{5,18},{6,22},{7,26},{9,3},{10,7},{11,11... | collective-permute-start | bytes 12296 | tf_op jit(solution)/shard_map/ppermute | solution.py:515
  57.5 1.0 %shard_map.105 = f32[8,6,8,512]{3,2,1,0:T(8,128)} custom-call(f32[8,6,8,512]{3,2,1,0:T(8,128)S(1)} %get-tuple-element.56.refs_0_, f32[8,512]{1,0:T(8,128)S(1)} %shard_map.104.refs_1_.refs_2_, f32[8,6,8,128]{3,2,1,0:T(8,128)S(1)} %get-tuple-element.58.refs_2_, f32[8,6,8,128]{3,2,1,0:T(8,128)S(1)} %collective-permute-done.13.refs_3_, ...), custom_call_target="tpu_custom_call" | custom-call | tf_op jit(solution)/shard_map/pallas_call | solution.py:406
  58.5 2.3 %collective-permute-done.20.beyond_ref = f32[8,128]{1,0:T(8,128)S(1)} collective-permute-done((f32[8,128]{1,0:T(8,128)S(1)}, f32[8,128]{1,0:T(8,128)S(1)}, u32[]{:S(2)}, u32[]{:S(2)}) %collective-permute-start.20) | collective-permute-done | bytes 4128 | tf_op jit(solution)/shard_map/ppermute | solution.py:515
  (39 shorter events, 7.9 us)
Async XLA Ops:
  1.9 8.5 %collective-permute-start.2 = (f32[8,6,8,128]{3,2,1,0:T(8,128)S(1)}, f32[8,6,8,128]{3,2,1,0:T(8,128)S(1)}, u32[]{:S(2)}, u32[]{:S(2)}) collective-permute-start(f32[8,6,8,128]{3,2,1,0:T(8,128)S(1)} %get-tuple-element.43), channel_id=1, source_target_pairs={{0,8},{8,0},{16,24},{24,16},{1,9},{9,1},{17,25},{25,17},{2,10},{10... | collective-permute-start | bytes 589832 | tf_op jit(solution)/shard_map/ppermute | solution.py:449
  3.2 7.2 %collective-permute-start.3 = (f32[8,6,8,128]{3,2,1,0:T(8,128)S(1)}, f32[8,6,8,128]{3,2,1,0:T(8,128)S(1)}, u32[]{:S(2)}, u32[]{:S(2)}) collective-permute-start(f32[8,6,8,128]{3,2,1,0:T(8,128)S(1)} %get-tuple-element.44), channel_id=1, source_target_pairs={{0,16},{8,24},{16,0},{24,8},{1,17},{9,25},{17,1},{25,9},{2,18},{10... | collective-permute-start | bytes 589832 | tf_op jit(solution)/shard_map/ppermute | solution.py:449
  4.5 8.6 %collective-permute-start.4 = (f32[8,6,8,128]{3,2,1,0:T(8,128)S(1)}, f32[8,6,8,128]{3,2,1,0:T(8,128)S(1)}, u32[]{:S(2)}, u32[]{:S(2)}) collective-permute-start(f32[8,6,8,128]{3,2,1,0:T(8,128)S(1)} %get-tuple-element.45), channel_id=1, source_target_pairs={{0,24},{8,16},{16,8},{24,0},{1,25},{9,17},{17,9},{25,1},{2,26},{10... | collective-permute-start | bytes 589832 | tf_op jit(solution)/shard_map/ppermute | solution.py:449
  4.8 11.6 %collective-permute-start = (f32[8,6,8,128]{3,2,1,0:T(8,128)S(1)}, f32[8,6,8,128]{3,2,1,0:T(8,128)S(1)}, u32[]{:S(2)}, u32[]{:S(2)}) collective-permute-start(f32[8,6,8,128]{3,2,1,0:T(8,128)S(1)} %get-tuple-element.34), channel_id=1, source_target_pairs={{0,1},{1,2},{2,3},{3,4},{4,5},{5,6},{6,7},{7,0},{8,9},{9,10},{10,1... | collective-permute-start | bytes 589832 | tf_op jit(solution)/shard_map/ppermute | solution.py:455
  7.5 8.8 %collective-permute-start.1 = (f32[8,6,8,128]{3,2,1,0:T(8,128)S(1)}, f32[8,6,8,128]{3,2,1,0:T(8,128)S(1)}, u32[]{:S(2)}, u32[]{:S(2)}) collective-permute-start(f32[8,6,8,128]{3,2,1,0:T(8,128)S(1)} %get-tuple-element.35), channel_id=1, source_target_pairs={{1,0},{2,1},{3,2},{4,3},{5,4},{6,5},{7,6},{0,7},{9,8},{10,9},{11,1... | collective-permute-start | bytes 589832 | tf_op jit(solution)/shard_map/ppermute | solution.py:456
  13.6 6.9 %collective-permute-start.5 = (f32[8,6,8,128]{3,2,1,0:T(8,128)S(1)}, f32[8,6,8,128]{3,2,1,0:T(8,128)S(1)}, u32[]{:S(2)}, u32[]{:S(2)}) collective-permute-start(f32[8,6,8,128]{3,2,1,0:T(8,128)S(1)} %get-tuple-element.47.refs_6_), channel_id=1, source_target_pairs={{0,8},{8,0},{16,24},{24,16},{1,9},{9,1},{17,25},{25,17},{2,10},{10... | collective-permute-start | bytes 589832 | tf_op jit(solution)/shard_map/ppermute | solution.py:449
  14.9 7.7 %collective-permute-start.6 = (f32[8,6,8,128]{3,2,1,0:T(8,128)S(1)}, f32[8,6,8,128]{3,2,1,0:T(8,128)S(1)}, u32[]{:S(2)}, u32[]{:S(2)}) collective-permute-start(f32[8,6,8,128]{3,2,1,0:T(8,128)S(1)} %get-tuple-element.48.refs_7_), channel_id=1, source_target_pairs={{0,16},{8,24},{16,0},{24,8},{1,17},{9,25},{17,1},{25,9},{2,18},{10... | collective-permute-start | bytes 589832 | tf_op jit(solution)/shard_map/ppermute | solution.py:449
  15.2 7.4 %collective-permute-start.7 = (f32[8,6,8,128]{3,2,1,0:T(8,128)S(1)}, f32[8,6,8,128]{3,2,1,0:T(8,128)S(1)}, u32[]{:S(2)}, u32[]{:S(2)}) collective-permute-start(f32[8,6,8,128]{3,2,1,0:T(8,128)S(1)} %get-tuple-element.49.refs_8_), channel_id=1, source_target_pairs={{0,24},{8,16},{16,8},{24,0},{1,25},{9,17},{17,9},{25,1},{2,26},{10... | collective-permute-start | bytes 589832 | tf_op jit(solution)/shard_map/ppermute | solution.py:449
  19.0 11.0 %collective-permute-start.10 = (f32[8,6,8,128]{3,2,1,0:T(8,128)S(1)}, f32[8,6,8,128]{3,2,1,0:T(8,128)S(1)}, u32[]{:S(2)}, u32[]{:S(2)}) collective-permute-start(f32[8,6,8,128]{3,2,1,0:T(8,128)S(1)} %get-tuple-element.39.refs_1_), channel_id=1, source_target_pairs={{0,8},{8,0},{16,24},{24,16},{1,9},{9,1},{17,25},{25,17},{2,10},{10... | collective-permute-start | bytes 589832 | tf_op jit(solution)/shard_map/ppermute | solution.py:449
  20.3 11.1 %collective-permute-start.11 = (f32[8,6,8,128]{3,2,1,0:T(8,128)S(1)}, f32[8,6,8,128]{3,2,1,0:T(8,128)S(1)}, u32[]{:S(2)}, u32[]{:S(2)}) collective-permute-start(f32[8,6,8,128]{3,2,1,0:T(8,128)S(1)} %get-tuple-element.40.refs_2_), channel_id=1, source_target_pairs={{0,16},{8,24},{16,0},{24,8},{1,17},{9,25},{17,1},{25,9},{2,18},{10... | collective-permute-start | bytes 589832 | tf_op jit(solution)/shard_map/ppermute | solution.py:449
  20.5 10.8 %collective-permute-start.12 = (f32[8,6,8,128]{3,2,1,0:T(8,128)S(1)}, f32[8,6,8,128]{3,2,1,0:T(8,128)S(1)}, u32[]{:S(2)}, u32[]{:S(2)}) collective-permute-start(f32[8,6,8,128]{3,2,1,0:T(8,128)S(1)} %get-tuple-element.41.refs_3_), channel_id=1, source_target_pairs={{0,24},{8,16},{16,8},{24,0},{1,25},{9,17},{17,9},{25,1},{2,26},{10... | collective-permute-start | bytes 589832 | tf_op jit(solution)/shard_map/ppermute | solution.py:449
  22.8 13.3 %copy-start = (f32[8,6,8,512]{3,2,1,0:T(8,128)S(1)}, f32[8,6,8,512]{3,2,1,0:T(8,128)}, u32[]{:S(2)}) copy-start(f32[8,6,8,512]{3,2,1,0:T(8,128)} %refs_1_.2) | copy-start | bytes 2359300
  22.8 13.1 %collective-permute-start.8 = (f32[8,6,8,128]{3,2,1,0:T(8,128)S(1)}, f32[8,6,8,128]{3,2,1,0:T(8,128)S(1)}, u32[]{:S(2)}, u32[]{:S(2)}) collective-permute-start(f32[8,6,8,128]{3,2,1,0:T(8,128)S(1)} %get-tuple-element.51), channel_id=1, source_target_pairs={{0,1},{1,2},{2,3},{3,4},{4,5},{5,6},{6,7},{7,0},{8,9},{9,10},{10,1... | collective-permute-start | bytes 589832 | tf_op jit(solution)/shard_map/ppermute | solution.py:455
  30.0 6.1 %collective-permute-start.9 = (f32[8,6,8,128]{3,2,1,0:T(8,128)S(1)}, f32[8,6,8,128]{3,2,1,0:T(8,128)S(1)}, u32[]{:S(2)}, u32[]{:S(2)}) collective-permute-start(f32[8,6,8,128]{3,2,1,0:T(8,128)S(1)} %get-tuple-element.52), channel_id=1, source_target_pairs={{1,0},{2,1},{3,2},{4,3},{5,4},{6,5},{7,6},{0,7},{9,8},{10,9},{11,1... | collective-permute-start | bytes 589832 | tf_op jit(solution)/shard_map/ppermute | solution.py:456
  32.0 5.2 %collective-permute-start.13 = (f32[8,6,8,128]{3,2,1,0:T(8,128)S(1)}, f32[8,6,8,128]{3,2,1,0:T(8,128)S(1)}, u32[]{:S(2)}, u32[]{:S(2)}) collective-permute-start(f32[8,6,8,128]{3,2,1,0:T(8,128)S(1)} %get-tuple-element.59), channel_id=1, source_target_pairs={{0,8},{8,0},{16,24},{24,16},{1,9},{9,1},{17,25},{25,17},{2,10},{10... | collective-permute-start | bytes 589832 | tf_op jit(solution)/shard_map/ppermute | solution.py:449
  32.7 7.1 %collective-permute-start.14 = (f32[8,6,8,128]{3,2,1,0:T(8,128)S(1)}, f32[8,6,8,128]{3,2,1,0:T(8,128)S(1)}, u32[]{:S(2)}, u32[]{:S(2)}) collective-permute-start(f32[8,6,8,128]{3,2,1,0:T(8,128)S(1)} %get-tuple-element.60), channel_id=1, source_target_pairs={{0,16},{8,24},{16,0},{24,8},{1,17},{9,25},{17,1},{25,9},{2,18},{10... | collective-permute-start | bytes 589832 | tf_op jit(solution)/shard_map/ppermute | solution.py:449
  34.4 6.6 %collective-permute-start.15 = (f32[8,6,8,128]{3,2,1,0:T(8,128)S(1)}, f32[8,6,8,128]{3,2,1,0:T(8,128)S(1)}, u32[]{:S(2)}, u32[]{:S(2)}) collective-permute-start(f32[8,6,8,128]{3,2,1,0:T(8,128)S(1)} %get-tuple-element.61), channel_id=1, source_target_pairs={{0,24},{8,16},{16,8},{24,0},{1,25},{9,17},{17,9},{25,1},{2,26},{10... | collective-permute-start | bytes 589832 | tf_op jit(solution)/shard_map/ppermute | solution.py:449
  35.9 8.2 %copy-start.1 = (f32[8,512,128]{2,1,0:T(8,128)S(1)}, f32[8,512,128]{2,1,0:T(8,128)}, u32[]{:S(2)}) copy-start(f32[8,512,128]{2,1,0:T(8,128)} %mode_ref.1) | copy-start | bytes 6291460
  37.2 9.0 %copy-start.2 = (s32[8,512]{1,0:T(8,128)S(1)}, s32[8,512]{1,0:T(8,128)}, u32[]{:S(2)}) copy-start(s32[8,512]{1,0:T(8,128)} %refs_1_.3) | copy-start | bytes 49156
  41.4 3.1 %collective-permute-start.16 = (f32[8,512]{1,0:T(8,128)S(1)}, f32[8,512]{1,0:T(8,128)S(1)}, u32[]{:S(2)}, u32[]{:S(2)}) collective-permute-start(f32[8,512]{1,0:T(8,128)S(1)} %shard_map.104.refs_1_.refs_2_), channel_id=1, source_target_pairs={{0,8},{8,0},{16,24},{24,16},{1,9},{9,1},{17,25},{25,17},{2,10},{10... | collective-permute-start | bytes 49160 | tf_op jit(solution)/shard_map/ppermute | solution.py:449
  42.2 2.6 %collective-permute-start.17 = (f32[8,512]{1,0:T(8,128)S(1)}, f32[8,512]{1,0:T(8,128)S(1)}, u32[]{:S(2)}, u32[]{:S(2)}) collective-permute-start(f32[8,512]{1,0:T(8,128)S(1)} %shard_map.104.refs_1_.refs_2_), channel_id=1, source_target_pairs={{0,16},{8,24},{16,0},{24,8},{1,17},{9,25},{17,1},{25,9},{2,18},{10... | collective-permute-start | bytes 49160 | tf_op jit(solution)/shard_map/ppermute | solution.py:449
  42.7 3.5 %collective-permute-start.18 = (f32[8,512]{1,0:T(8,128)S(1)}, f32[8,512]{1,0:T(8,128)S(1)}, u32[]{:S(2)}, u32[]{:S(2)}) collective-permute-start(f32[8,512]{1,0:T(8,128)S(1)} %shard_map.104.refs_1_.refs_2_), channel_id=1, source_target_pairs={{0,24},{8,16},{16,8},{24,0},{1,25},{9,17},{17,9},{25,1},{2,26},{10... | collective-permute-start | bytes 49160 | tf_op jit(solution)/shard_map/ppermute | solution.py:449
  46.7 11.8 %collective-permute-start.19 = (f32[8,128]{1,0:T(8,128)S(1)}, f32[8,128]{1,0:T(8,128)S(1)}, u32[]{:S(2)}, u32[]{:S(2)}) collective-permute-start(f32[8,128]{1,0:T(8,128)S(1)} %get-tuple-element.62), channel_id=1, source_target_pairs={{0,3},{1,7},{2,9},{3,14},{4,18},{5,21},{6,27},{7,31},{8,2},{9,6},{... | collective-permute-start | bytes 12296 | tf_op jit(solution)/shard_map/ppermute | solution.py:515
  55.6 5.2 %collective-permute-start.20 = (f32[8,128]{1,0:T(8,128)S(1)}, f32[8,128]{1,0:T(8,128)S(1)}, u32[]{:S(2)}, u32[]{:S(2)}) collective-permute-start(f32[8,128]{1,0:T(8,128)S(1)} %get-tuple-element.63), channel_id=1, source_target_pairs={{1,2},{2,6},{3,10},{4,14},{5,18},{6,22},{7,26},{9,3},{10,7},{11,11... | collective-permute-start | bytes 12296 | tf_op jit(solution)/shard_map/ppermute | solution.py:515
